TPU v7x, 256 devices: a whole 4x4x8 slice. The times are simulated.
256 devices in a mesh: blk: 16 (over x_lo, y, core), rep: 16 (over z, x_hi).
Axes of the slice: x: 4 (x_hi: 2, x_lo: 2; x = x_hi * 2 + x_lo), y: 4, z: 8, core: 2. Of those that a mesh axis runs over, the one named last changes fastest.
Arguments:
- stale: bfloat16 [32768, 512], P(('blk', 'rep')), may hold values from -6 to 6
- w_self: bfloat16 [512, 512], replicated, may hold values from -0.25 to 0.25
- w_neigh: bfloat16 [512, 512], replicated, may hold values from -6 to 6
- tile_weights: bfloat16 [16, 16, 16, 12, 128, 128], P('blk', 'rep'), may hold values from 0 to 4, as said below
- tile_pos: int32 [16, 16, 16, 12], P('blk', 'rep'), may hold values from 0 to 15, as said below
- tile_counts: int32 [16, 16, 16], P('blk', 'rep'), may hold values from 0 to 12, as said below
Outputs:
- refreshed: bfloat16 [32768, 512], P(('blk', 'rep'))
Inputs may be any that keep to these rules, and one draw needn't show every extreme that they name: `tile_weights`: non-negative edge weights. `tile_pos`: distinct within the live head of every list. `tile_counts`: every device has one full list.
All inputs are finite; a program needn't handle non-finite values.
Results may differ from a plain program's by a relative error of at most 0.013.
Values may be sent and summed in bfloat16 or wider, within the bound.
No kernel may reach another device: no remote copies, remote signals or barrier semaphores. Data moves between devices by JAX's collectives and lax.ppermute only.
A program may use at most 64 MiB of HBM per device.

v0:
```python
import functools

import jax
import jax.numpy as jnp
from jax import lax
from jax.experimental import pallas as pl
from jax.experimental.pallas import tpu as pltpu
from jax.sharding import PartitionSpec as P


TILE = 128
PAIRS = (((1, 2), (0, 1), (1, 3)), ((0, 2), (1, 1), (0, 3)))
SINGLE = (1, 0)


def blk_at(index, dx, dy, dc):
    x, y, c = index >> 3, (index >> 1) & 3, index & 1
    return (((x + dx) & 1) << 3) | (((y + dy) & 3) << 1) | ((c + dc) & 1)


def rep_at(index, dz, dx):
    return (((index >> 1) + dz) % 8) * 2 + ((index & 1) + dx) % 2


def from_pair(value, index):
    pairs = [(blk_at(i, *PAIRS[i & 1][index], 0), i) for i in range(16)]
    return lax.ppermute(value, "blk", pairs)


def from_single(value):
    return lax.ppermute(value, "blk", [(blk_at(i, *SINGLE, 0), i) for i in range(16)])


def from_other_core(value):
    return lax.ppermute(value, "blk", [(i, i ^ 1) for i in range(16)])


def to_rep(value, dz, dx):
    pairs = [
        (b * 16 + i, b * 16 + rep_at(i, -dz if b & 1 else dz, dx))
        for b in range(16)
        for i in range(16)
    ]
    return lax.ppermute(value, ("blk", "rep"), pairs)


def slot_sources(blk):
    def fetched(dc):
        found = []
        for index in range(3):
            for other in range(2):
                options = [blk_at(blk, *offsets[index], dc + other) for offsets in PAIRS]
                found.append(jnp.where(((blk + dc) & 1) == 0, *options))
        return found

    one = [blk_at(blk, *SINGLE, dc) for dc in range(2)]
    own = [blk_at(blk, 0, 0, dc) for dc in range(2)]
    return own + fetched(0) + one[:1] + fetched(1) + one[1:]


def place_kernel(meta, counts_hbm, places_hbm, tiles_ref, a_ref, counts, places, table_sems, sems):
    tables = [
        pltpu.make_async_copy(counts_hbm, counts, table_sems.at[0]),
        pltpu.make_async_copy(places_hbm, places, table_sems.at[1]),
    ]
    for table in tables:
        table.start()
    blk, my_z, my_x = meta[0], meta[1] >> 1, meta[1] & 1
    sign = 1 - 2 * (blk & 1)
    sources = slot_sources(blk)
    for slot, source in enumerate(sources):
        a_ref[slot] = jnp.zeros(a_ref.shape[1:], a_ref.dtype)
        if slot == 0:
            for table in tables:
                table.wait()

        def start(k, carry):
            place = places[k, 0, source]
            row = (((((place >> 1) - my_z) * sign) & 7) << 1) | ((place ^ my_x) & 1)
            span = pl.ds(pl.multiple_of(row * TILE, TILE), TILE)
            pltpu.make_async_copy(
                tiles_ref.at[source, k], a_ref.at[slot, span, :], sems.at[slot, k]
            ).start()
            return carry

        lax.fori_loop(0, counts[source], start, 0)
    for slot, source in enumerate(sources):

        def wait(k, carry):
            pltpu.make_async_copy(
                tiles_ref.at[0, 0], a_ref.at[slot, :TILE, :], sems.at[slot, k]
            ).wait()
            return carry

        lax.fori_loop(0, counts[source], wait, 0)


def place_tiles(meta, counts, places, tiles):
    lists, cap = tiles.shape[:2]
    whole = pl.BlockSpec(memory_space=pl.ANY)
    hbm = [pltpu.with_memory_space_constraint(x, pltpu.HBM) for x in (counts, places, tiles)]
    return pl.pallas_call(
        place_kernel,
        in_specs=[pl.BlockSpec(memory_space=pltpu.SMEM), whole, whole, whole],
        out_specs=pl.BlockSpec(memory_space=pltpu.VMEM),
        out_shape=pltpu.VMEM((lists, 16 * TILE, TILE), jnp.bfloat16),
        scratch_shapes=[
            pltpu.SMEM(counts.shape, jnp.int32),
            pltpu.SMEM(places.shape, jnp.int32),
            pltpu.SemaphoreType.DMA((2,)),
            pltpu.SemaphoreType.DMA((lists, cap)),
        ],
        compiler_params=pltpu.CompilerParams(vmem_limit_bytes=1 << 20),
        cost_estimate=pl.CostEstimate(flops=1 << 20, transcendentals=0, bytes_accessed=14 << 20),
        name="place_tiles",
    )(meta, *hbm)


def near_kernel(first, a_ref, *refs):
    out_ref = refs[-1]
    sources, partials = refs[:2], refs[2:-1]
    right = jnp.concatenate([ref[...] for ref in sources], axis=0)
    for slot in range(out_ref.shape[0]):
        span = slice(slot * 2 * TILE, (slot + 1) * 2 * TILE)
        left = jnp.concatenate([a_ref[first + j, span, :] for j in range(4)], axis=1)
        result = jnp.dot(left, right, preferred_element_type=jnp.float32)
        for partial in partials:
            result += partial[slot]
        out_ref[slot] = result


def near_sums(first, a, sources, *partials):
    vmem = pl.BlockSpec(memory_space=pltpu.VMEM)
    width = sources[0].shape[1]
    return pl.pallas_call(
        functools.partial(near_kernel, first),
        in_specs=[vmem] * (3 + len(partials)),
        out_specs=vmem,
        out_shape=pltpu.VMEM((8, 2 * TILE, width), jnp.float32),
        compiler_params=pltpu.CompilerParams(vmem_limit_bytes=4 << 20),
        cost_estimate=pl.CostEstimate(
            flops=2 * 2048 * 512 * width, transcendentals=0, bytes_accessed=6 << 20
        ),
        name="near_sums",
    )(a, *sources, *partials)


def far_kernel(slots, planes, meta, a_ref, partial_ref, *refs):
    my_z = meta[1] >> 1
    sources, out_refs = refs[:4], refs[4:]
    width = sources[0].shape[-1]
    right = jnp.concatenate([ref[...] for ref in sources], axis=0)
    mine = lax.broadcasted_iota(jnp.int32, (8, TILE), 0) == my_z
    diagonal = lax.broadcasted_iota(jnp.int32, (TILE, TILE), 0) == lax.broadcasted_iota(
        jnp.int32, (TILE, TILE), 1
    )
    out_refs = list(out_refs)
    for slot in slots:
        first, rows = planes[0] * TILE, len(planes) * TILE
        span = slice(slot * 2 * TILE + first, slot * 2 * TILE + first + rows)
        pieces = [a_ref[j, span, :] for j in range(a_ref.shape[0])]
        weight = jnp.zeros((rows, TILE), jnp.float32)
        for piece in pieces:
            weight += piece.astype(jnp.float32)
        left = jnp.concatenate(pieces[8:], axis=1)
        result = partial_ref[slot, first : first + rows] + jnp.dot(
            left, right, preferred_element_type=jnp.float32
        )
        degree = jnp.sum(weight, axis=1, keepdims=True)
        for x in range(len(planes)):
            out_ref = out_refs.pop(0)
            part = slice(x * TILE, (x + 1) * TILE)
            out_ref[:TILE, :] = result[part].astype(out_ref.dtype)
            deg = jnp.sum(jnp.where(diagonal, degree[part], 0.0), axis=0, keepdims=True)
            deg = jnp.where(mine, deg, 0.0)
            pad = jnp.zeros((8, width - TILE), jnp.float32)
            out_ref[TILE:, :] = jnp.concatenate([deg, pad], axis=1).astype(out_ref.dtype)


def far_sums(slots, planes, meta, a, partial, *sources):
    width = sources[0].shape[1]
    vmem = pl.BlockSpec(memory_space=pltpu.VMEM)
    outs = len(planes) * len(slots)
    return pl.pallas_call(
        functools.partial(far_kernel, slots, planes),
        in_specs=[pl.BlockSpec(memory_space=pltpu.SMEM)] + [vmem] * 6,
        out_specs=[vmem] * outs,
        out_shape=[jax.ShapeDtypeStruct((TILE + 8, width), jnp.bfloat16)] * outs,
        compiler_params=pltpu.CompilerParams(vmem_limit_bytes=8 << 20),
        cost_estimate=pl.CostEstimate(
            flops=outs * 2 * TILE * 1024 * width, transcendentals=0, bytes_accessed=outs << 19
        ),
        name="far_sums",
    )(meta, a, partial, *sources)


def prepare_kernel(stale_ref, w_self_ref, *refs):
    hidden_ref, total_ref = refs[-2:]
    stale = stale_ref[...]
    hidden_ref[...] = jnp.dot(stale, w_self_ref[...], preferred_element_type=jnp.float32)
    total = sum(ref[...].astype(jnp.float32) for ref in refs[:-2])
    total_ref[:TILE, :] = total[:TILE] + stale.astype(jnp.float32)
    total_ref[TILE:, :] = total[TILE:]


def prepare(stale, w_self, *parts):
    rows, width = parts[0].shape
    return pl.pallas_call(
        prepare_kernel,
        out_shape=[
            jax.ShapeDtypeStruct(stale.shape, jnp.float32),
            jax.ShapeDtypeStruct((rows, width), jnp.float32),
        ],
        compiler_params=pltpu.CompilerParams(vmem_limit_bytes=4 << 20),
        name="prepare",
    )(stale, w_self, *parts)


def finish_kernel(hidden_ref, total_ref, other_ref, w_neigh_ref, out_ref):
    total = total_ref[...] + other_ref[...].astype(jnp.float32)
    degree = jnp.sum(total[TILE:, :TILE], axis=0, keepdims=True)
    degree = jnp.broadcast_to(degree, (TILE, TILE)).T
    degree = jnp.concatenate([degree] * (total.shape[1] // TILE), axis=1)
    mean = (total[:TILE] / (1.0 + degree)).astype(jnp.bfloat16)
    hidden = hidden_ref[...] + jnp.dot(
        mean, w_neigh_ref[...], preferred_element_type=jnp.float32
    )
    active = jnp.maximum(hidden, 0.0)
    out = active * lax.rsqrt(jnp.mean(active * active, axis=-1, keepdims=True) + 1e-05)
    out_ref[...] = out.astype(out_ref.dtype)


def finish(hidden, total, other, w_neigh):
    return pl.pallas_call(
        finish_kernel,
        out_shape=jax.ShapeDtypeStruct(hidden.shape, jnp.bfloat16),
        compiler_params=pltpu.CompilerParams(vmem_limit_bytes=4 << 20),
        name="finish",
    )(hidden, total, other, w_neigh)


def refresh(stale, w_self, w_neigh, tile_weights, tile_pos, tile_counts):
    meta = jnp.stack([lax.axis_index("blk"), lax.axis_index("rep")]).astype(jnp.int32)
    places = jnp.transpose(tile_pos, (0, 3, 1, 2))[0]
    mate = from_other_core(stale)
    single = from_single(stale)
    own_pair = jnp.concatenate([stale, mate], axis=0)
    received = []
    for index in range(3):
        received.append(from_pair(own_pair, index))
    a = place_tiles(meta, tile_counts[0, 0], places, tile_weights[0, 0])
    first, second, third = received
    first, a = lax.optimization_barrier((first, a))
    first_far = from_other_core(first)
    partial = near_sums(0, a, (own_pair, first))
    second, third, single, partial = lax.optimization_barrier((second, third, single, partial))
    second_far = from_other_core(second)
    late_far = from_other_core(jnp.concatenate([third, single], axis=0))
    partial = near_sums(4, a, (second, third), partial)
    args = (meta, a, partial, single, first_far, second_far, late_far)
    both = (0, 1)

    def hop(value, dz, dx=0):
        return to_rep(value, dz, dx)

    own, other = far_sums((4,), both, *args)
    up_other = hop(other, 1)
    down_own = hop(own, -1)
    three_own, three_other, five_own, five_other = far_sums((3, 5), both, *args)
    down_other = hop(five_other, -1)
    up_own = hop(three_own, 1)
    up_other = hop(three_other + up_other, 1)
    down_own = hop(five_own + down_own, -1)
    for slots in ((2, 6), (1, 7)):
        low_own, low_other, high_own, high_other = far_sums(slots, both, *args)
        down_other = hop(high_other + down_other, -1)
        up_own = hop(low_own + up_own, 1)
        up_other = hop(low_other + up_other, 1)
        down_own = hop(high_own + down_own, -1)
    (other,) = far_sums((0,), (1,), *args)
    other = sum(part.astype(jnp.float32) for part in (other, up_other, down_other))
    other = hop(other.astype(jnp.bfloat16), 0, 1)
    (own,) = far_sums((0,), (0,), *args)
    hidden, total = prepare(stale, w_self, own, up_own, down_own)
    return finish(hidden, total, other, w_neigh)


def solution(mesh):
    return jax.shard_map(
        refresh,
        mesh=mesh,
        in_specs=(
            P(("blk", "rep"), None),
            P(),
            P(),
            P("blk", "rep", None, None, None, None),
            P("blk", "rep", None, None),
            P("blk", "rep", None),
        ),
        out_specs=P(("blk", "rep"), None),
        check_vma=False,
    )
```

profile of v0, /device:TPU:8, one launch (start us, length us, event | category | flops | bytes accessed | tf_op | source)
XLA Modules:
  0.0 61.1 jit_solution(4997126322765304304)
XLA Ops:
  1.6 3.3 %collective-permute-start.1 = (bf16[256,512]{1,0:T(8,128)(2,1)S(1)}, bf16[256,512]{1,0:T(8,128)(2,1)S(1)}, u32[]{:S(2)}, u32[]{:S(2)}) collective-permute-start(bf16[256,512]{1,0:T(8,128)(2,1)S(1)} %constant_dynamic-update-slice_fusion.refs_0_), channel_id=1, source_target_pairs={{192,0},{80,16},{224,32},{112,48},{128,64},{16,80},{160,96},{48,11... | collective-permute-start | bytes 786440 | tf_op jit(solution)/shard_map/ppermute | solution.py:27
  4.9 1.3 %collective-permute-start.3 = (bf16[256,512]{1,0:T(8,128)(2,1)S(1)}, bf16[256,512]{1,0:T(8,128)(2,1)S(1)}, u32[]{:S(2)}, u32[]{:S(2)}) collective-permute-start(bf16[256,512]{1,0:T(8,128)(2,1)S(1)} %constant_dynamic-update-slice_fusion.refs_0_), channel_id=1, source_target_pairs={{224,0},{112,16},{128,32},{16,48},{160,64},{48,80},{192,96},{80,11... | collective-permute-start | bytes 786440 | tf_op jit(solution)/shard_map/ppermute | solution.py:27
  6.9 1.5 %collective-permute-start.4 = (bf16[128,512]{1,0:T(8,128)(2,1)}, bf16[128,512]{1,0:T(8,128)(2,1)S(1)}, u32[]{:S(2)}, u32[]{:S(2)}) collective-permute-start(bf16[128,512]{1,0:T(8,128)(2,1)} %stale_ref.1), channel_id=1, source_target_pairs={{128,0},{144,16},{160,32},{176,48},{192,64},{208,80},{224,96},{240... | collective-permute-start | bytes 393224 | tf_op jit(solution)/shard_map/ppermute | solution.py:31
  8.4 6.4 %place_tiles.1.a_ref = bf16[16,2048,128]{2,1,0:T(8,128)(2,1)S(1)} custom-call(s32[2]{0:T(128)S(1)} %pad_add_fusion.meta, s32[16]{0:T(128)} %bitcast.9, s32[12,1,16]{2,1,0:T(1,128)} %bitcast.8, bf16[16,12,128,128]{3,2,1,0:T(8,128)(2,1)} %bitcast.7), custom_call_target="tpu_custom_call" | custom-call | flops 1048576 | bytes 14680064 | tf_op jit(solution)/shard_map/place_tiles/pallas_call | solution.py:102
  14.9 1.3 %near_sums.2.refs_2_ = f32[8,256,512]{2,1,0:T(8,128)S(1)} custom-call(bf16[16,2048,128]{2,1,0:T(8,128)(2,1)S(1)} %place_tiles.1.a_ref, bf16[256,512]{1,0:T(8,128)(2,1)S(1)} %constant_dynamic-update-slice_fusion.refs_0_, bf16[256,512]{1,0:T(8,128)(2,1)S(1)} %collective-permute-done.1.refs_1_), custom_call_target="tpu_custom_call" | custom-call | flops 1073741824 | bytes 6291456 | tf_op jit(solution)/shard_map/near_sums/pallas_call | solution.py:135
  16.1 2.1 %collective-permute-done.4.refs_0_ = bf16[128,512]{1,0:T(8,128)(2,1)S(1)} collective-permute-done((bf16[128,512]{1,0:T(8,128)(2,1)}, bf16[128,512]{1,0:T(8,128)(2,1)S(1)}, u32[]{:S(2)}, u32[]{:S(2)}) %collective-permute-start.4) | collective-permute-done | bytes 131104 | tf_op jit(solution)/shard_map/ppermute | solution.py:31
  19.0 1.3 %near_sums.3.partial_ref = f32[8,256,512]{2,1,0:T(8,128)S(1)} custom-call(bf16[16,2048,128]{2,1,0:T(8,128)(2,1)S(1)} %place_tiles.1.a_ref, bf16[256,512]{1,0:T(8,128)(2,1)S(1)} %collective-permute-done.2.refs_0_, bf16[256,512]{1,0:T(8,128)(2,1)S(1)} %collective-permute-done.3.refs_1_, f32[8,256,512]{2,1,0:T(8,128)S(1)} %near_sums.2.refs_2_), custom_call_target="tpu_custom_call" | custom-call | flops 1073741824 | bytes 6291456 | tf_op jit(solution)/shard_map/near_sums/pallas_call | solution.py:135
  21.8 2.0 %collective-permute-start.15 = (bf16[136,512]{1,0:T(8,128)(2,1)S(1)}, bf16[136,512]{1,0:T(8,128)(2,1)S(1)}, u32[]{:S(2)}, u32[]{:S(2)}) collective-permute-start(bf16[136,512]{1,0:T(8,128)(2,1)S(1)} %get-tuple-element.45), channel_id=1, source_target_pairs={{0,2},{1,3},{2,4},{3,5},{4,6},{5,7},{6,8},{7,9},{8,10},{9,11},{10,... | collective-permute-start | bytes 417800 | tf_op jit(solution)/shard_map/ppermute | solution.py:44
  23.8 4.0 %collective-permute-start.11 = (bf16[136,512]{1,0:T(8,128)(2,1)S(1)}, bf16[136,512]{1,0:T(8,128)(2,1)S(1)}, u32[]{:S(2)}, u32[]{:S(2)}) collective-permute-start(bf16[136,512]{1,0:T(8,128)(2,1)S(1)} %get-tuple-element.39), channel_id=1, source_target_pairs={{0,14},{1,15},{2,0},{3,1},{4,2},{5,3},{6,4},{7,5},{8,6},{9,7},{10,... | collective-permute-start | bytes 417800 | tf_op jit(solution)/shard_map/ppermute | solution.py:44
  27.9 1.3 %far_sums.9 = (bf16[136,512]{1,0:T(8,128)(2,1)S(1)}, bf16[136,512]{1,0:T(8,128)(2,1)S(1)}, bf16[136,512]{1,0:T(8,128)(2,1)S(1)}, bf16[136,512]{1,0:T(8,128)(2,1)S(1)}) custom-call(s32[2]{0:T(128)S(1)} %pad_add_fusion.meta, bf16[16,2048,128]{2,1,0:T(8,128)(2,1)S(1)} %place_tiles.1.a_ref, f32[8,256,512]{2,1,0:T(8,128)S(1)} %near_sums.3.partial_ref, ...), custom_call_target="tpu_custom_call" | custom-call | flops 536870912 | bytes 2097152 | tf_op jit(solution)/shard_map/far_sums/pallas_call | solution.py:184
  29.2 2.0 %collective-permute-start.19 = (bf16[136,512]{1,0:T(8,128)(2,1)S(1)}, bf16[136,512]{1,0:T(8,128)(2,1)S(1)}, u32[]{:S(2)}, u32[]{:S(2)}) collective-permute-start(bf16[136,512]{1,0:T(8,128)(2,1)S(1)} %get-tuple-element.48), channel_id=1, source_target_pairs={{0,14},{1,15},{2,0},{3,1},{4,2},{5,3},{6,4},{7,5},{8,6},{9,7},{10,... | collective-permute-start | bytes 417800 | tf_op jit(solution)/shard_map/ppermute | solution.py:44
  31.9 1.3 %far_sums.8 = (bf16[136,512]{1,0:T(8,128)(2,1)S(1)}, bf16[136,512]{1,0:T(8,128)(2,1)S(1)}, bf16[136,512]{1,0:T(8,128)(2,1)S(1)}, bf16[136,512]{1,0:T(8,128)(2,1)S(1)}) custom-call(s32[2]{0:T(128)S(1)} %pad_add_fusion.meta, bf16[16,2048,128]{2,1,0:T(8,128)(2,1)S(1)} %place_tiles.1.a_ref, f32[8,256,512]{2,1,0:T(8,128)S(1)} %near_sums.3.partial_ref, ...), custom_call_target="tpu_custom_call" | custom-call | flops 536870912 | bytes 2097152 | tf_op jit(solution)/shard_map/far_sums/pallas_call | solution.py:184
  33.2 3.0 %collective-permute-start.12 = (bf16[136,512]{1,0:T(8,128)(2,1)S(1)}, bf16[136,512]{1,0:T(8,128)(2,1)S(1)}, u32[]{:S(2)}, u32[]{:S(2)}) collective-permute-start(bf16[136,512]{1,0:T(8,128)(2,1)S(1)} %add.38), channel_id=1, source_target_pairs={{0,14},{1,15},{2,0},{3,1},{4,2},{5,3},{6,4},{7,5},{8,6},{9,7},{10,... | collective-permute-start | bytes 417800 | tf_op jit(solution)/shard_map/ppermute | solution.py:44
  36.3 2.0 %collective-permute-start.20 = (bf16[136,512]{1,0:T(8,128)(2,1)S(1)}, bf16[136,512]{1,0:T(8,128)(2,1)S(1)}, u32[]{:S(2)}, u32[]{:S(2)}) collective-permute-start(bf16[136,512]{1,0:T(8,128)(2,1)S(1)} %add.45), channel_id=1, source_target_pairs={{0,14},{1,15},{2,0},{3,1},{4,2},{5,3},{6,4},{7,5},{8,6},{9,7},{10,... | collective-permute-start | bytes 417800 | tf_op jit(solution)/shard_map/ppermute | solution.py:44
  38.5 1.3 %far_sums.7 = (bf16[136,512]{1,0:T(8,128)(2,1)S(1)}, bf16[136,512]{1,0:T(8,128)(2,1)S(1)}, bf16[136,512]{1,0:T(8,128)(2,1)S(1)}, bf16[136,512]{1,0:T(8,128)(2,1)S(1)}) custom-call(s32[2]{0:T(128)S(1)} %pad_add_fusion.meta, bf16[16,2048,128]{2,1,0:T(8,128)(2,1)S(1)} %place_tiles.1.a_ref, f32[8,256,512]{2,1,0:T(8,128)S(1)} %near_sums.3.partial_ref, ...), custom_call_target="tpu_custom_call" | custom-call | flops 536870912 | bytes 2097152 | tf_op jit(solution)/shard_map/far_sums/pallas_call | solution.py:184
  39.8 1.7 %collective-permute-start.9 = (bf16[136,512]{1,0:T(8,128)(2,1)S(1)}, bf16[136,512]{1,0:T(8,128)(2,1)S(1)}, u32[]{:S(2)}, u32[]{:S(2)}) collective-permute-start(bf16[136,512]{1,0:T(8,128)(2,1)S(1)} %add.36), channel_id=1, source_target_pairs={{0,2},{1,3},{2,4},{3,5},{4,6},{5,7},{6,8},{7,9},{8,10},{9,11},{10,... | collective-permute-start | bytes 417800 | tf_op jit(solution)/shard_map/ppermute | solution.py:44
  41.5 2.5 %collective-permute-start.13 = (bf16[136,512]{1,0:T(8,128)(2,1)S(1)}, bf16[136,512]{1,0:T(8,128)(2,1)S(1)}, u32[]{:S(2)}, u32[]{:S(2)}) collective-permute-start(bf16[136,512]{1,0:T(8,128)(2,1)S(1)} %add.39), channel_id=1, source_target_pairs={{0,14},{1,15},{2,0},{3,1},{4,2},{5,3},{6,4},{7,5},{8,6},{9,7},{10,... | collective-permute-start | bytes 417800 | tf_op jit(solution)/shard_map/ppermute | solution.py:44
  44.1 2.1 %collective-permute-start.21 = (bf16[136,512]{1,0:T(8,128)(2,1)S(1)}, bf16[136,512]{1,0:T(8,128)(2,1)S(1)}, u32[]{:S(2)}, u32[]{:S(2)}) collective-permute-start(bf16[136,512]{1,0:T(8,128)(2,1)S(1)} %add.46), channel_id=1, source_target_pairs={{0,14},{1,15},{2,0},{3,1},{4,2},{5,3},{6,4},{7,5},{8,6},{9,7},{10,... | collective-permute-start | bytes 417800 | tf_op jit(solution)/shard_map/ppermute | solution.py:44
  47.2 1.3 %collective-permute-done.9 = bf16[136,512]{1,0:T(8,128)(2,1)S(1)} collective-permute-done((bf16[136,512]{1,0:T(8,128)(2,1)S(1)}, bf16[136,512]{1,0:T(8,128)(2,1)S(1)}, u32[]{:S(2)}, u32[]{:S(2)}) %collective-permute-start.9) | collective-permute-done | bytes 139296 | tf_op jit(solution)/shard_map/ppermute | solution.py:44
  49.2 2.7 %collective-permute-start.14 = (bf16[136,512]{1,0:T(8,128)(2,1)S(1)}, bf16[136,512]{1,0:T(8,128)(2,1)S(1)}, u32[]{:S(2)}, u32[]{:S(2)}) collective-permute-start(bf16[136,512]{1,0:T(8,128)(2,1)S(1)} %add.40), channel_id=1, source_target_pairs={{0,14},{1,15},{2,0},{3,1},{4,2},{5,3},{6,4},{7,5},{8,6},{9,7},{10,... | collective-permute-start | bytes 417800 | tf_op jit(solution)/shard_map/ppermute | solution.py:44
  51.9 1.4 %collective-permute-done.18 = bf16[136,512]{1,0:T(8,128)(2,1)S(1)} collective-permute-done((bf16[136,512]{1,0:T(8,128)(2,1)S(1)}, bf16[136,512]{1,0:T(8,128)(2,1)S(1)}, u32[]{:S(2)}, u32[]{:S(2)}) %collective-permute-start.18) | collective-permute-done | bytes 139296 | tf_op jit(solution)/shard_map/ppermute | solution.py:44
  53.4 3.1 %collective-permute-start.22 = (bf16[136,512]{1,0:T(8,128)(2,1)S(1)}, bf16[136,512]{1,0:T(8,128)(2,1)S(1)}, u32[]{:S(2)}, u32[]{:S(2)}) collective-permute-start(bf16[136,512]{1,0:T(8,128)(2,1)S(1)} %add_convert_fusion), channel_id=1, source_target_pairs={{0,1},{1,0},{2,3},{3,2},{4,5},{5,4},{6,7},{7,6},{8,9},{9,8},{10,11... | collective-permute-start | bytes 417800 | tf_op jit(solution)/shard_map/ppermute | solution.py:44
  57.6 2.5 %collective-permute-done.22.other_ref = bf16[136,512]{1,0:T(8,128)(2,1)S(1)} collective-permute-done((bf16[136,512]{1,0:T(8,128)(2,1)S(1)}, bf16[136,512]{1,0:T(8,128)(2,1)S(1)}, u32[]{:S(2)}, u32[]{:S(2)}) %collective-permute-start.22) | collective-permute-done | bytes 139296 | tf_op jit(solution)/shard_map/ppermute | solution.py:44
  60.1 1.1 %finish.1 = bf16[128,512]{1,0:T(8,128)(2,1)} custom-call(f32[128,512]{1,0:T(8,128)S(1)} %get-tuple-element.40.hidden_ref, f32[136,512]{1,0:T(8,128)S(1)} %get-tuple-element.41.total_ref, bf16[136,512]{1,0:T(8,128)(2,1)S(1)} %collective-permute-done.22.other_ref, bf16[512,512]{1,0:T(8,128)(2,1)S(1)} %copy-done.1), custom_call_target="tpu_custom_call" | custom-call | tf_op jit(solution)/shard_map/finish/pallas_call | solution.py:234
  (54 shorter events, 8.6 us)
Async XLA Ops:
  0.0 1.6 %collective-permute-start = (bf16[128,512]{1,0:T(8,128)(2,1)}, bf16[128,512]{1,0:T(8,128)(2,1)S(1)}, u32[]{:S(2)}, u32[]{:S(2)}) collective-permute-start(bf16[128,512]{1,0:T(8,128)(2,1)} %stale_ref.1), channel_id=1, source_target_pairs={{0,16},{16,0},{32,48},{48,32},{64,80},{80,64},{96,112},{112,96},{1... | collective-permute-start | bytes 393224 | tf_op jit(solution)/shard_map/ppermute | solution.py:35
  1.6 13.3 %collective-permute-start.1 = (bf16[256,512]{1,0:T(8,128)(2,1)S(1)}, bf16[256,512]{1,0:T(8,128)(2,1)S(1)}, u32[]{:S(2)}, u32[]{:S(2)}) collective-permute-start(bf16[256,512]{1,0:T(8,128)(2,1)S(1)} %constant_dynamic-update-slice_fusion.refs_0_), channel_id=1, source_target_pairs={{192,0},{80,16},{224,32},{112,48},{128,64},{16,80},{160,96},{48,11... | collective-permute-start | bytes 786440 | tf_op jit(solution)/shard_map/ppermute | solution.py:27
  4.9 13.4 %collective-permute-start.3 = (bf16[256,512]{1,0:T(8,128)(2,1)S(1)}, bf16[256,512]{1,0:T(8,128)(2,1)S(1)}, u32[]{:S(2)}, u32[]{:S(2)}) collective-permute-start(bf16[256,512]{1,0:T(8,128)(2,1)S(1)} %constant_dynamic-update-slice_fusion.refs_0_), channel_id=1, source_target_pairs={{224,0},{112,16},{128,32},{16,48},{160,64},{48,80},{192,96},{80,11... | collective-permute-start | bytes 786440 | tf_op jit(solution)/shard_map/ppermute | solution.py:27
  6.2 12.1 %collective-permute-start.2 = (bf16[256,512]{1,0:T(8,128)(2,1)S(1)}, bf16[256,512]{1,0:T(8,128)(2,1)S(1)}, u32[]{:S(2)}, u32[]{:S(2)}) collective-permute-start(bf16[256,512]{1,0:T(8,128)(2,1)S(1)} %constant_dynamic-update-slice_fusion.refs_0_), channel_id=1, source_target_pairs={{32,0},{176,16},{64,32},{208,48},{96,64},{240,80},{0,96},{144,112}... | collective-permute-start | bytes 786440 | tf_op jit(solution)/shard_map/ppermute | solution.py:27
  6.9 11.4 %collective-permute-start.4 = (bf16[128,512]{1,0:T(8,128)(2,1)}, bf16[128,512]{1,0:T(8,128)(2,1)S(1)}, u32[]{:S(2)}, u32[]{:S(2)}) collective-permute-start(bf16[128,512]{1,0:T(8,128)(2,1)} %stale_ref.1), channel_id=1, source_target_pairs={{128,0},{144,16},{160,32},{176,48},{192,64},{208,80},{224,96},{240... | collective-permute-start | bytes 393224 | tf_op jit(solution)/shard_map/ppermute | solution.py:31
  18.3 2.6 %collective-permute-start.7 = (bf16[384,512]{1,0:T(8,128)(2,1)S(1)}, bf16[384,512]{1,0:T(8,128)(2,1)S(1)}, u32[]{:S(2)}, u32[]{:S(2)}) collective-permute-start(bf16[384,512]{1,0:T(8,128)(2,1)S(1)} %pad_maximum_fusion), channel_id=1, source_target_pairs={{0,16},{16,0},{32,48},{48,32},{64,80},{80,64},{96,112},{112,96},{1... | collective-permute-start | bytes 1179656 | tf_op jit(solution)/shard_map/ppermute | solution.py:35
  18.4 2.1 %collective-permute-start.5 = (bf16[256,512]{1,0:T(8,128)(2,1)S(1)}, bf16[256,512]{1,0:T(8,128)(2,1)S(1)}, u32[]{:S(2)}, u32[]{:S(2)}) collective-permute-start(bf16[256,512]{1,0:T(8,128)(2,1)S(1)} %collective-permute-done.1.refs_1_), channel_id=1, source_target_pairs={{0,16},{16,0},{32,48},{48,32},{64,80},{80,64},{96,112},{112,96},{1... | collective-permute-start | bytes 786440 | tf_op jit(solution)/shard_map/ppermute | solution.py:35
  18.9 2.0 %collective-permute-start.6 = (bf16[256,512]{1,0:T(8,128)(2,1)S(1)}, bf16[256,512]{1,0:T(8,128)(2,1)S(1)}, u32[]{:S(2)}, u32[]{:S(2)}) collective-permute-start(bf16[256,512]{1,0:T(8,128)(2,1)S(1)} %collective-permute-done.2.refs_0_), channel_id=1, source_target_pairs={{0,16},{16,0},{32,48},{48,32},{64,80},{80,64},{96,112},{112,96},{1... | collective-permute-start | bytes 786440 | tf_op jit(solution)/shard_map/ppermute | solution.py:35
  21.8 9.3 %collective-permute-start.15 = (bf16[136,512]{1,0:T(8,128)(2,1)S(1)}, bf16[136,512]{1,0:T(8,128)(2,1)S(1)}, u32[]{:S(2)}, u32[]{:S(2)}) collective-permute-start(bf16[136,512]{1,0:T(8,128)(2,1)S(1)} %get-tuple-element.45), channel_id=1, source_target_pairs={{0,2},{1,3},{2,4},{3,5},{4,6},{5,7},{6,8},{7,9},{8,10},{9,11},{10,... | collective-permute-start | bytes 417800 | tf_op jit(solution)/shard_map/ppermute | solution.py:44
  23.8 9.3 %collective-permute-start.11 = (bf16[136,512]{1,0:T(8,128)(2,1)S(1)}, bf16[136,512]{1,0:T(8,128)(2,1)S(1)}, u32[]{:S(2)}, u32[]{:S(2)}) collective-permute-start(bf16[136,512]{1,0:T(8,128)(2,1)S(1)} %get-tuple-element.39), channel_id=1, source_target_pairs={{0,14},{1,15},{2,0},{3,1},{4,2},{5,3},{6,4},{7,5},{8,6},{9,7},{10,... | collective-permute-start | bytes 417800 | tf_op jit(solution)/shard_map/ppermute | solution.py:44
  29.2 7.1 %collective-permute-start.19 = (bf16[136,512]{1,0:T(8,128)(2,1)S(1)}, bf16[136,512]{1,0:T(8,128)(2,1)S(1)}, u32[]{:S(2)}, u32[]{:S(2)}) collective-permute-start(bf16[136,512]{1,0:T(8,128)(2,1)S(1)} %get-tuple-element.48), channel_id=1, source_target_pairs={{0,14},{1,15},{2,0},{3,1},{4,2},{5,3},{6,4},{7,5},{8,6},{9,7},{10,... | collective-permute-start | bytes 417800 | tf_op jit(solution)/shard_map/ppermute | solution.py:44
  31.2 7.1 %collective-permute-start.16 = (bf16[136,512]{1,0:T(8,128)(2,1)S(1)}, bf16[136,512]{1,0:T(8,128)(2,1)S(1)}, u32[]{:S(2)}, u32[]{:S(2)}) collective-permute-start(bf16[136,512]{1,0:T(8,128)(2,1)S(1)} %add.41), channel_id=1, source_target_pairs={{0,2},{1,3},{2,4},{3,5},{4,6},{5,7},{6,8},{7,9},{8,10},{9,11},{10,... | collective-permute-start | bytes 417800 | tf_op jit(solution)/shard_map/ppermute | solution.py:44
  31.6 8.2 %collective-permute-start.8 = (bf16[136,512]{1,0:T(8,128)(2,1)S(1)}, bf16[136,512]{1,0:T(8,128)(2,1)S(1)}, u32[]{:S(2)}, u32[]{:S(2)}) collective-permute-start(bf16[136,512]{1,0:T(8,128)(2,1)S(1)} %get-tuple-element.35), channel_id=1, source_target_pairs={{0,2},{1,3},{2,4},{3,5},{4,6},{5,7},{6,8},{7,9},{8,10},{9,11},{10,... | collective-permute-start | bytes 417800 | tf_op jit(solution)/shard_map/ppermute | solution.py:44
  33.2 8.3 %collective-permute-start.12 = (bf16[136,512]{1,0:T(8,128)(2,1)S(1)}, bf16[136,512]{1,0:T(8,128)(2,1)S(1)}, u32[]{:S(2)}, u32[]{:S(2)}) collective-permute-start(bf16[136,512]{1,0:T(8,128)(2,1)S(1)} %add.38), channel_id=1, source_target_pairs={{0,14},{1,15},{2,0},{3,1},{4,2},{5,3},{6,4},{7,5},{8,6},{9,7},{10,... | collective-permute-start | bytes 417800 | tf_op jit(solution)/shard_map/ppermute | solution.py:44
  36.3 7.8 %collective-permute-start.20 = (bf16[136,512]{1,0:T(8,128)(2,1)S(1)}, bf16[136,512]{1,0:T(8,128)(2,1)S(1)}, u32[]{:S(2)}, u32[]{:S(2)}) collective-permute-start(bf16[136,512]{1,0:T(8,128)(2,1)S(1)} %add.45), channel_id=1, source_target_pairs={{0,14},{1,15},{2,0},{3,1},{4,2},{5,3},{6,4},{7,5},{8,6},{9,7},{10,... | collective-permute-start | bytes 417800 | tf_op jit(solution)/shard_map/ppermute | solution.py:44
  38.3 7.9 %collective-permute-start.17 = (bf16[136,512]{1,0:T(8,128)(2,1)S(1)}, bf16[136,512]{1,0:T(8,128)(2,1)S(1)}, u32[]{:S(2)}, u32[]{:S(2)}) collective-permute-start(bf16[136,512]{1,0:T(8,128)(2,1)S(1)} %add.42), channel_id=1, source_target_pairs={{0,2},{1,3},{2,4},{3,5},{4,6},{5,7},{6,8},{7,9},{8,10},{9,11},{10,... | collective-permute-start | bytes 417800 | tf_op jit(solution)/shard_map/ppermute | solution.py:44
  39.8 8.6 %collective-permute-start.9 = (bf16[136,512]{1,0:T(8,128)(2,1)S(1)}, bf16[136,512]{1,0:T(8,128)(2,1)S(1)}, u32[]{:S(2)}, u32[]{:S(2)}) collective-permute-start(bf16[136,512]{1,0:T(8,128)(2,1)S(1)} %add.36), channel_id=1, source_target_pairs={{0,2},{1,3},{2,4},{3,5},{4,6},{5,7},{6,8},{7,9},{8,10},{9,11},{10,... | collective-permute-start | bytes 417800 | tf_op jit(solution)/shard_map/ppermute | solution.py:44
  41.5 7.6 %collective-permute-start.13 = (bf16[136,512]{1,0:T(8,128)(2,1)S(1)}, bf16[136,512]{1,0:T(8,128)(2,1)S(1)}, u32[]{:S(2)}, u32[]{:S(2)}) collective-permute-start(bf16[136,512]{1,0:T(8,128)(2,1)S(1)} %add.39), channel_id=1, source_target_pairs={{0,14},{1,15},{2,0},{3,1},{4,2},{5,3},{6,4},{7,5},{8,6},{9,7},{10,... | collective-permute-start | bytes 417800 | tf_op jit(solution)/shard_map/ppermute | solution.py:44
  44.1 7.8 %collective-permute-start.21 = (bf16[136,512]{1,0:T(8,128)(2,1)S(1)}, bf16[136,512]{1,0:T(8,128)(2,1)S(1)}, u32[]{:S(2)}, u32[]{:S(2)}) collective-permute-start(bf16[136,512]{1,0:T(8,128)(2,1)S(1)} %add.46), channel_id=1, source_target_pairs={{0,14},{1,15},{2,0},{3,1},{4,2},{5,3},{6,4},{7,5},{8,6},{9,7},{10,... | collective-permute-start | bytes 417800 | tf_op jit(solution)/shard_map/ppermute | solution.py:44
  46.2 7.1 %collective-permute-start.18 = (bf16[136,512]{1,0:T(8,128)(2,1)S(1)}, bf16[136,512]{1,0:T(8,128)(2,1)S(1)}, u32[]{:S(2)}, u32[]{:S(2)}) collective-permute-start(bf16[136,512]{1,0:T(8,128)(2,1)S(1)} %add.43), channel_id=1, source_target_pairs={{0,2},{1,3},{2,4},{3,5},{4,6},{5,7},{6,8},{7,9},{8,10},{9,11},{10,... | collective-permute-start | bytes 417800 | tf_op jit(solution)/shard_map/ppermute | solution.py:44
  48.5 8.8 %collective-permute-start.10 = (bf16[136,512]{1,0:T(8,128)(2,1)S(1)}, bf16[136,512]{1,0:T(8,128)(2,1)S(1)}, u32[]{:S(2)}, u32[]{:S(2)}) collective-permute-start(bf16[136,512]{1,0:T(8,128)(2,1)S(1)} %add.37), channel_id=1, source_target_pairs={{0,2},{1,3},{2,4},{3,5},{4,6},{5,7},{6,8},{7,9},{8,10},{9,11},{10,... | collective-permute-start | bytes 417800 | tf_op jit(solution)/shard_map/ppermute | solution.py:44
  49.2 8.1 %collective-permute-start.14 = (bf16[136,512]{1,0:T(8,128)(2,1)S(1)}, bf16[136,512]{1,0:T(8,128)(2,1)S(1)}, u32[]{:S(2)}, u32[]{:S(2)}) collective-permute-start(bf16[136,512]{1,0:T(8,128)(2,1)S(1)} %add.40), channel_id=1, source_target_pairs={{0,14},{1,15},{2,0},{3,1},{4,2},{5,3},{6,4},{7,5},{8,6},{9,7},{10,... | collective-permute-start | bytes 417800 | tf_op jit(solution)/shard_map/ppermute | solution.py:44
  53.4 6.7 %copy-start.1 = (bf16[512,512]{1,0:T(8,128)(2,1)S(1)}, bf16[512,512]{1,0:T(8,128)(2,1)}, u32[]{:S(2)}) copy-start(bf16[512,512]{1,0:T(8,128)(2,1)} %w_neigh_ref.1) | copy-start | bytes 1572868
  53.4 6.6 %collective-permute-start.22 = (bf16[136,512]{1,0:T(8,128)(2,1)S(1)}, bf16[136,512]{1,0:T(8,128)(2,1)S(1)}, u32[]{:S(2)}, u32[]{:S(2)}) collective-permute-start(bf16[136,512]{1,0:T(8,128)(2,1)S(1)} %add_convert_fusion), channel_id=1, source_target_pairs={{0,1},{1,0},{2,3},{3,2},{4,5},{5,4},{6,7},{7,6},{8,9},{9,8},{10,11... | collective-permute-start | bytes 417800 | tf_op jit(solution)/shard_map/ppermute | solution.py:44
  (2 other events, 7.9 us)
where the time goes:
time: 62.3 us; the launch traced here: 61.1 us
  starting transfers between devices  34.2 us (55%)
  Pallas kernels  16.8 us (27%)
  waiting for transfers between devices  8.45 us (14%)
  local copies, waits for them, and re-layouts  0.94 us (2%)
    ppermute x15, starting transfers between devices, to_rep(): return lax.ppermute(value, ('blk', 'rep'), pairs)  26.7 us
    pallas_call x6, Pallas kernels, far_sums(): pl.pallas_call(functools.partial(far_kernel, slots, planes), in_specs=[pl...  6.56 us
    pallas_call x1, Pallas kernels, place_tiles(): pl.pallas_call(place_kernel, in_specs=[pl.BlockSpec(memory_space=pltpu.SM...  6.39 us
    ppermute x3, starting transfers between devices, from_pair(): return lax.ppermute(value, 'blk', pairs)  5.31 us
    ppermute x15, waiting for transfers between devices, to_rep(): return lax.ppermute(value, ('blk', 'rep'), pairs)  5.13 us
    pallas_call x2, Pallas kernels, near_sums(): pl.pallas_call(functools.partial(near_kernel, first), in_specs=[vmem] * (...  2.56 us
    ppermute x1, waiting for transfers between devices, from_single(): lax.ppermute(value, 'blk', [(blk_at(i, *SINGLE, 0), i) for i in range(16)])  2.11 us
    ppermute x1, starting transfers between devices, from_single(): lax.ppermute(value, 'blk', [(blk_at(i, *SINGLE, 0), i) for i in range(16)])  1.49 us
  transfers between devices with their start and end apart: 23, of which 7 were waited for; matrix products, arithmetic and copies ran while one was open for 2% of the time, Pallas kernels for 24%

commit v1 on v0

--- a/solution.py
+++ b/solution.py
@@ -9,8 +9,8 @@
 
 
 TILE = 128
-PAIRS = (((1, 2), (0, 1), (1, 3)), ((0, 2), (1, 1), (0, 3)))
-SINGLE = (1, 0)
+PAIRS = (((1, 0), (0, 2), (1, 1)), ((0, 1), (1, 3), (0, 3)))
+SINGLE = (1, 2)
 
 
 def blk_at(index, dx, dy, dc):
@@ -218,10 +218,10 @@
 
 def finish_kernel(hidden_ref, total_ref, other_ref, w_neigh_ref, out_ref):
     total = total_ref[...] + other_ref[...].astype(jnp.float32)
-    degree = jnp.sum(total[TILE:, :TILE], axis=0, keepdims=True)
-    degree = jnp.broadcast_to(degree, (TILE, TILE)).T
-    degree = jnp.concatenate([degree] * (total.shape[1] // TILE), axis=1)
-    mean = (total[:TILE] / (1.0 + degree)).astype(jnp.bfloat16)
+    scale = 1.0 / (1.0 + jnp.sum(total[TILE:, :TILE], axis=0, keepdims=True))
+    scale = jnp.broadcast_to(scale, (TILE, TILE)).T
+    scale = jnp.concatenate([scale] * (total.shape[1] // TILE), axis=1)
+    mean = (total[:TILE] * scale).astype(jnp.bfloat16)
     hidden = hidden_ref[...] + jnp.dot(
         mean, w_neigh_ref[...], preferred_element_type=jnp.float32
     )

time: 62.3 us -> 62.1 us (level)
  starting transfers between devices: 34.2 us -> 33.4 us
    ppermute x3, starting transfers between devices: 5.31 us -> 4.58 us  [from_pair(): return lax.ppermute(value, 'blk', pairs)]
    ppermute x15, starting transfers between devices: 26.7 us -> 26 us  [to_rep(): return lax.ppermute(value, ('blk', 'rep'), pairs)]
    ppermute x1, starting transfers between devices: 1.49 us -> 2.18 us  [from_single(): lax.ppermute(value, 'blk', [(blk_at(i, *SINGLE, 0), i) for i in range(16)])]
  transfers between devices with their start and end apart: 23 -> 23, of which waited for: 7 -> 8; matrix products, arithmetic and copies ran while one was open for 2% -> 2% of each run, Pallas kernels for 24% -> 24%
where the time goes in v1:
time: 62.1 us; the launch traced here: 60.9 us
  starting transfers between devices  33.4 us (54%)
  Pallas kernels  16.7 us (27%)
  waiting for transfers between devices  9.06 us (15%)
  local copies, waits for them, and re-layouts  0.94 us (2%)
    ppermute x15, starting transfers between devices, to_rep(): return lax.ppermute(value, ('blk', 'rep'), pairs)  26 us
    pallas_call x6, Pallas kernels, far_sums(): pl.pallas_call(functools.partial(far_kernel, slots, planes), in_specs=[pl...  6.56 us
    pallas_call x1, Pallas kernels, place_tiles(): pl.pallas_call(place_kernel, in_specs=[pl.BlockSpec(memory_space=pltpu.SM...  6.27 us
    ppermute x15, waiting for transfers between devices, to_rep(): return lax.ppermute(value, ('blk', 'rep'), pairs)  5.06 us
    ppermute x3, starting transfers between devices, from_pair(): return lax.ppermute(value, 'blk', pairs)  4.58 us
    pallas_call x2, Pallas kernels, near_sums(): pl.pallas_call(functools.partial(near_kernel, first), in_specs=[vmem] * (...  2.56 us
    ppermute x1, waiting for transfers between devices, from_single(): lax.ppermute(value, 'blk', [(blk_at(i, *SINGLE, 0), i) for i in range(16)])  2.32 us
    ppermute x1, starting transfers between devices, from_single(): lax.ppermute(value, 'blk', [(blk_at(i, *SINGLE, 0), i) for i in range(16)])  2.18 us
  transfers between devices with their start and end apart: 23, of which 8 were waited for; matrix products, arithmetic and copies ran while one was open for 2% of the time, Pallas kernels for 24%

profile of v1, /device:TPU:8, one launch (start us, length us, event | category | flops | bytes accessed | tf_op | source)
XLA Modules:
  0.0 60.9 jit_solution(4842216414203160565)
XLA Ops:
  1.6 1.6 %collective-permute-start.1 = (bf16[256,512]{1,0:T(8,128)(2,1)S(1)}, bf16[256,512]{1,0:T(8,128)(2,1)S(1)}, u32[]{:S(2)}, u32[]{:S(2)}) collective-permute-start(bf16[256,512]{1,0:T(8,128)(2,1)S(1)} %constant_dynamic-update-slice_fusion.refs_0_), channel_id=1, source_target_pairs={{128,0},{48,16},{160,32},{80,48},{192,64},{112,80},{224,96},{16,11... | collective-permute-start | bytes 786440 | tf_op jit(solution)/shard_map/ppermute | solution.py:27
  3.1 2.1 %collective-permute-start.3 = (bf16[256,512]{1,0:T(8,128)(2,1)S(1)}, bf16[256,512]{1,0:T(8,128)(2,1)S(1)}, u32[]{:S(2)}, u32[]{:S(2)}) collective-permute-start(bf16[256,512]{1,0:T(8,128)(2,1)S(1)} %constant_dynamic-update-slice_fusion.refs_0_), channel_id=1, source_target_pairs={{160,0},{112,16},{192,32},{16,48},{224,64},{48,80},{128,96},{80,11... | collective-permute-start | bytes 786440 | tf_op jit(solution)/shard_map/ppermute | solution.py:27
  6.2 2.2 %collective-permute-start.4 = (bf16[128,512]{1,0:T(8,128)(2,1)}, bf16[128,512]{1,0:T(8,128)(2,1)S(1)}, u32[]{:S(2)}, u32[]{:S(2)}) collective-permute-start(bf16[128,512]{1,0:T(8,128)(2,1)} %stale_ref.1), channel_id=1, source_target_pairs={{192,0},{208,16},{224,32},{240,48},{128,64},{144,80},{160,96},{176... | collective-permute-start | bytes 393224 | tf_op jit(solution)/shard_map/ppermute | solution.py:31
  8.4 6.3 %place_tiles.1.a_ref = bf16[16,2048,128]{2,1,0:T(8,128)(2,1)S(1)} custom-call(s32[2]{0:T(128)S(1)} %pad_add_fusion.meta, s32[16]{0:T(128)} %bitcast.9, s32[12,1,16]{2,1,0:T(1,128)} %bitcast.8, bf16[16,12,128,128]{3,2,1,0:T(8,128)(2,1)} %bitcast.7), custom_call_target="tpu_custom_call" | custom-call | flops 1048576 | bytes 14680064 | tf_op jit(solution)/shard_map/place_tiles/pallas_call | solution.py:102
  14.7 1.3 %near_sums.2.refs_2_ = f32[8,256,512]{2,1,0:T(8,128)S(1)} custom-call(bf16[16,2048,128]{2,1,0:T(8,128)(2,1)S(1)} %place_tiles.1.a_ref, bf16[256,512]{1,0:T(8,128)(2,1)S(1)} %constant_dynamic-update-slice_fusion.refs_0_, bf16[256,512]{1,0:T(8,128)(2,1)S(1)} %collective-permute-done.1.refs_1_), custom_call_target="tpu_custom_call" | custom-call | flops 1073741824 | bytes 6291456 | tf_op jit(solution)/shard_map/near_sums/pallas_call | solution.py:135
  16.0 2.3 %collective-permute-done.4.refs_0_ = bf16[128,512]{1,0:T(8,128)(2,1)S(1)} collective-permute-done((bf16[128,512]{1,0:T(8,128)(2,1)}, bf16[128,512]{1,0:T(8,128)(2,1)S(1)}, u32[]{:S(2)}, u32[]{:S(2)}) %collective-permute-start.4) | collective-permute-done | bytes 131104 | tf_op jit(solution)/shard_map/ppermute | solution.py:31
  19.5 1.3 %near_sums.3.partial_ref = f32[8,256,512]{2,1,0:T(8,128)S(1)} custom-call(bf16[16,2048,128]{2,1,0:T(8,128)(2,1)S(1)} %place_tiles.1.a_ref, bf16[256,512]{1,0:T(8,128)(2,1)S(1)} %collective-permute-done.2.refs_0_, bf16[256,512]{1,0:T(8,128)(2,1)S(1)} %collective-permute-done.3.refs_1_, f32[8,256,512]{2,1,0:T(8,128)S(1)} %near_sums.2.refs_2_), custom_call_target="tpu_custom_call" | custom-call | flops 1073741824 | bytes 6291456 | tf_op jit(solution)/shard_map/near_sums/pallas_call | solution.py:135
  22.4 1.4 %collective-permute-start.15 = (bf16[136,512]{1,0:T(8,128)(2,1)S(1)}, bf16[136,512]{1,0:T(8,128)(2,1)S(1)}, u32[]{:S(2)}, u32[]{:S(2)}) collective-permute-start(bf16[136,512]{1,0:T(8,128)(2,1)S(1)} %get-tuple-element.45), channel_id=1, source_target_pairs={{0,2},{1,3},{2,4},{3,5},{4,6},{5,7},{6,8},{7,9},{8,10},{9,11},{10,... | collective-permute-start | bytes 417800 | tf_op jit(solution)/shard_map/ppermute | solution.py:44
  23.8 4.0 %collective-permute-start.11 = (bf16[136,512]{1,0:T(8,128)(2,1)S(1)}, bf16[136,512]{1,0:T(8,128)(2,1)S(1)}, u32[]{:S(2)}, u32[]{:S(2)}) collective-permute-start(bf16[136,512]{1,0:T(8,128)(2,1)S(1)} %get-tuple-element.39), channel_id=1, source_target_pairs={{0,14},{1,15},{2,0},{3,1},{4,2},{5,3},{6,4},{7,5},{8,6},{9,7},{10,... | collective-permute-start | bytes 417800 | tf_op jit(solution)/shard_map/ppermute | solution.py:44
  27.8 1.3 %far_sums.9 = (bf16[136,512]{1,0:T(8,128)(2,1)S(1)}, bf16[136,512]{1,0:T(8,128)(2,1)S(1)}, bf16[136,512]{1,0:T(8,128)(2,1)S(1)}, bf16[136,512]{1,0:T(8,128)(2,1)S(1)}) custom-call(s32[2]{0:T(128)S(1)} %pad_add_fusion.meta, bf16[16,2048,128]{2,1,0:T(8,128)(2,1)S(1)} %place_tiles.1.a_ref, f32[8,256,512]{2,1,0:T(8,128)S(1)} %near_sums.3.partial_ref, ...), custom_call_target="tpu_custom_call" | custom-call | flops 536870912 | bytes 2097152 | tf_op jit(solution)/shard_map/far_sums/pallas_call | solution.py:184
  29.1 2.2 %collective-permute-start.19 = (bf16[136,512]{1,0:T(8,128)(2,1)S(1)}, bf16[136,512]{1,0:T(8,128)(2,1)S(1)}, u32[]{:S(2)}, u32[]{:S(2)}) collective-permute-start(bf16[136,512]{1,0:T(8,128)(2,1)S(1)} %get-tuple-element.48), channel_id=1, source_target_pairs={{0,14},{1,15},{2,0},{3,1},{4,2},{5,3},{6,4},{7,5},{8,6},{9,7},{10,... | collective-permute-start | bytes 417800 | tf_op jit(solution)/shard_map/ppermute | solution.py:44
  31.6 1.3 %far_sums.8 = (bf16[136,512]{1,0:T(8,128)(2,1)S(1)}, bf16[136,512]{1,0:T(8,128)(2,1)S(1)}, bf16[136,512]{1,0:T(8,128)(2,1)S(1)}, bf16[136,512]{1,0:T(8,128)(2,1)S(1)}) custom-call(s32[2]{0:T(128)S(1)} %pad_add_fusion.meta, bf16[16,2048,128]{2,1,0:T(8,128)(2,1)S(1)} %place_tiles.1.a_ref, f32[8,256,512]{2,1,0:T(8,128)S(1)} %near_sums.3.partial_ref, ...), custom_call_target="tpu_custom_call" | custom-call | flops 536870912 | bytes 2097152 | tf_op jit(solution)/shard_map/far_sums/pallas_call | solution.py:184
  33.0 3.2 %collective-permute-start.12 = (bf16[136,512]{1,0:T(8,128)(2,1)S(1)}, bf16[136,512]{1,0:T(8,128)(2,1)S(1)}, u32[]{:S(2)}, u32[]{:S(2)}) collective-permute-start(bf16[136,512]{1,0:T(8,128)(2,1)S(1)} %add.38), channel_id=1, source_target_pairs={{0,14},{1,15},{2,0},{3,1},{4,2},{5,3},{6,4},{7,5},{8,6},{9,7},{10,... | collective-permute-start | bytes 417800 | tf_op jit(solution)/shard_map/ppermute | solution.py:44
  36.2 2.0 %collective-permute-start.20 = (bf16[136,512]{1,0:T(8,128)(2,1)S(1)}, bf16[136,512]{1,0:T(8,128)(2,1)S(1)}, u32[]{:S(2)}, u32[]{:S(2)}) collective-permute-start(bf16[136,512]{1,0:T(8,128)(2,1)S(1)} %add.45), channel_id=1, source_target_pairs={{0,14},{1,15},{2,0},{3,1},{4,2},{5,3},{6,4},{7,5},{8,6},{9,7},{10,... | collective-permute-start | bytes 417800 | tf_op jit(solution)/shard_map/ppermute | solution.py:44
  38.4 1.3 %far_sums.7 = (bf16[136,512]{1,0:T(8,128)(2,1)S(1)}, bf16[136,512]{1,0:T(8,128)(2,1)S(1)}, bf16[136,512]{1,0:T(8,128)(2,1)S(1)}, bf16[136,512]{1,0:T(8,128)(2,1)S(1)}) custom-call(s32[2]{0:T(128)S(1)} %pad_add_fusion.meta, bf16[16,2048,128]{2,1,0:T(8,128)(2,1)S(1)} %place_tiles.1.a_ref, f32[8,256,512]{2,1,0:T(8,128)S(1)} %near_sums.3.partial_ref, ...), custom_call_target="tpu_custom_call" | custom-call | flops 536870912 | bytes 2097152 | tf_op jit(solution)/shard_map/far_sums/pallas_call | solution.py:184
  39.8 1.3 %collective-permute-start.9 = (bf16[136,512]{1,0:T(8,128)(2,1)S(1)}, bf16[136,512]{1,0:T(8,128)(2,1)S(1)}, u32[]{:S(2)}, u32[]{:S(2)}) collective-permute-start(bf16[136,512]{1,0:T(8,128)(2,1)S(1)} %add.36), channel_id=1, source_target_pairs={{0,2},{1,3},{2,4},{3,5},{4,6},{5,7},{6,8},{7,9},{8,10},{9,11},{10,... | collective-permute-start | bytes 417800 | tf_op jit(solution)/shard_map/ppermute | solution.py:44
  41.1 2.7 %collective-permute-start.13 = (bf16[136,512]{1,0:T(8,128)(2,1)S(1)}, bf16[136,512]{1,0:T(8,128)(2,1)S(1)}, u32[]{:S(2)}, u32[]{:S(2)}) collective-permute-start(bf16[136,512]{1,0:T(8,128)(2,1)S(1)} %add.39), channel_id=1, source_target_pairs={{0,14},{1,15},{2,0},{3,1},{4,2},{5,3},{6,4},{7,5},{8,6},{9,7},{10,... | collective-permute-start | bytes 417800 | tf_op jit(solution)/shard_map/ppermute | solution.py:44
  43.9 2.1 %collective-permute-start.21 = (bf16[136,512]{1,0:T(8,128)(2,1)S(1)}, bf16[136,512]{1,0:T(8,128)(2,1)S(1)}, u32[]{:S(2)}, u32[]{:S(2)}) collective-permute-start(bf16[136,512]{1,0:T(8,128)(2,1)S(1)} %add.46), channel_id=1, source_target_pairs={{0,14},{1,15},{2,0},{3,1},{4,2},{5,3},{6,4},{7,5},{8,6},{9,7},{10,... | collective-permute-start | bytes 417800 | tf_op jit(solution)/shard_map/ppermute | solution.py:44
  47.0 1.3 %collective-permute-done.9 = bf16[136,512]{1,0:T(8,128)(2,1)S(1)} collective-permute-done((bf16[136,512]{1,0:T(8,128)(2,1)S(1)}, bf16[136,512]{1,0:T(8,128)(2,1)S(1)}, u32[]{:S(2)}, u32[]{:S(2)}) %collective-permute-start.9) | collective-permute-done | bytes 139296 | tf_op jit(solution)/shard_map/ppermute | solution.py:44
  49.0 2.7 %collective-permute-start.14 = (bf16[136,512]{1,0:T(8,128)(2,1)S(1)}, bf16[136,512]{1,0:T(8,128)(2,1)S(1)}, u32[]{:S(2)}, u32[]{:S(2)}) collective-permute-start(bf16[136,512]{1,0:T(8,128)(2,1)S(1)} %add.40), channel_id=1, source_target_pairs={{0,14},{1,15},{2,0},{3,1},{4,2},{5,3},{6,4},{7,5},{8,6},{9,7},{10,... | collective-permute-start | bytes 417800 | tf_op jit(solution)/shard_map/ppermute | solution.py:44
  51.7 1.4 %collective-permute-done.18 = bf16[136,512]{1,0:T(8,128)(2,1)S(1)} collective-permute-done((bf16[136,512]{1,0:T(8,128)(2,1)S(1)}, bf16[136,512]{1,0:T(8,128)(2,1)S(1)}, u32[]{:S(2)}, u32[]{:S(2)}) %collective-permute-start.18) | collective-permute-done | bytes 139296 | tf_op jit(solution)/shard_map/ppermute | solution.py:44
  53.2 3.1 %collective-permute-start.22 = (bf16[136,512]{1,0:T(8,128)(2,1)S(1)}, bf16[136,512]{1,0:T(8,128)(2,1)S(1)}, u32[]{:S(2)}, u32[]{:S(2)}) collective-permute-start(bf16[136,512]{1,0:T(8,128)(2,1)S(1)} %add_convert_fusion), channel_id=1, source_target_pairs={{0,1},{1,0},{2,3},{3,2},{4,5},{5,4},{6,7},{7,6},{8,9},{9,8},{10,11... | collective-permute-start | bytes 417800 | tf_op jit(solution)/shard_map/ppermute | solution.py:44
  57.4 2.4 %collective-permute-done.22.other_ref = bf16[136,512]{1,0:T(8,128)(2,1)S(1)} collective-permute-done((bf16[136,512]{1,0:T(8,128)(2,1)S(1)}, bf16[136,512]{1,0:T(8,128)(2,1)S(1)}, u32[]{:S(2)}, u32[]{:S(2)}) %collective-permute-start.22) | collective-permute-done | bytes 139296 | tf_op jit(solution)/shard_map/ppermute | solution.py:44
  59.8 1.0 %finish.1 = bf16[128,512]{1,0:T(8,128)(2,1)} custom-call(f32[128,512]{1,0:T(8,128)S(1)} %get-tuple-element.40.hidden_ref, f32[136,512]{1,0:T(8,128)S(1)} %get-tuple-element.41.total_ref, bf16[136,512]{1,0:T(8,128)(2,1)S(1)} %collective-permute-done.22.other_ref, bf16[512,512]{1,0:T(8,128)(2,1)S(1)} %copy-done.1), custom_call_target="tpu_custom_call" | custom-call | tf_op jit(solution)/shard_map/finish/pallas_call | solution.py:234
  (54 shorter events, 8.9 us)
Async XLA Ops:
  0.0 1.6 %collective-permute-start = (bf16[128,512]{1,0:T(8,128)(2,1)}, bf16[128,512]{1,0:T(8,128)(2,1)S(1)}, u32[]{:S(2)}, u32[]{:S(2)}) collective-permute-start(bf16[128,512]{1,0:T(8,128)(2,1)} %stale_ref.1), channel_id=1, source_target_pairs={{0,16},{16,0},{32,48},{48,32},{64,80},{80,64},{96,112},{112,96},{1... | collective-permute-start | bytes 393224 | tf_op jit(solution)/shard_map/ppermute | solution.py:35
  1.6 13.1 %collective-permute-start.1 = (bf16[256,512]{1,0:T(8,128)(2,1)S(1)}, bf16[256,512]{1,0:T(8,128)(2,1)S(1)}, u32[]{:S(2)}, u32[]{:S(2)}) collective-permute-start(bf16[256,512]{1,0:T(8,128)(2,1)S(1)} %constant_dynamic-update-slice_fusion.refs_0_), channel_id=1, source_target_pairs={{128,0},{48,16},{160,32},{80,48},{192,64},{112,80},{224,96},{16,11... | collective-permute-start | bytes 786440 | tf_op jit(solution)/shard_map/ppermute | solution.py:27
  3.1 15.1 %collective-permute-start.3 = (bf16[256,512]{1,0:T(8,128)(2,1)S(1)}, bf16[256,512]{1,0:T(8,128)(2,1)S(1)}, u32[]{:S(2)}, u32[]{:S(2)}) collective-permute-start(bf16[256,512]{1,0:T(8,128)(2,1)S(1)} %constant_dynamic-update-slice_fusion.refs_0_), channel_id=1, source_target_pairs={{160,0},{112,16},{192,32},{16,48},{224,64},{48,80},{128,96},{80,11... | collective-permute-start | bytes 786440 | tf_op jit(solution)/shard_map/ppermute | solution.py:27
  5.3 13.5 %collective-permute-start.2 = (bf16[256,512]{1,0:T(8,128)(2,1)S(1)}, bf16[256,512]{1,0:T(8,128)(2,1)S(1)}, u32[]{:S(2)}, u32[]{:S(2)}) collective-permute-start(bf16[256,512]{1,0:T(8,128)(2,1)S(1)} %constant_dynamic-update-slice_fusion.refs_0_), channel_id=1, source_target_pairs={{64,0},{240,16},{96,32},{144,48},{0,64},{176,80},{32,96},{208,112}... | collective-permute-start | bytes 786440 | tf_op jit(solution)/shard_map/ppermute | solution.py:27
  6.2 12.1 %collective-permute-start.4 = (bf16[128,512]{1,0:T(8,128)(2,1)}, bf16[128,512]{1,0:T(8,128)(2,1)S(1)}, u32[]{:S(2)}, u32[]{:S(2)}) collective-permute-start(bf16[128,512]{1,0:T(8,128)(2,1)} %stale_ref.1), channel_id=1, source_target_pairs={{192,0},{208,16},{224,32},{240,48},{128,64},{144,80},{160,96},{176... | collective-permute-start | bytes 393224 | tf_op jit(solution)/shard_map/ppermute | solution.py:31
  18.8 2.6 %collective-permute-start.7 = (bf16[384,512]{1,0:T(8,128)(2,1)S(1)}, bf16[384,512]{1,0:T(8,128)(2,1)S(1)}, u32[]{:S(2)}, u32[]{:S(2)}) collective-permute-start(bf16[384,512]{1,0:T(8,128)(2,1)S(1)} %pad_maximum_fusion), channel_id=1, source_target_pairs={{0,16},{16,0},{32,48},{48,32},{64,80},{80,64},{96,112},{112,96},{1... | collective-permute-start | bytes 1179656 | tf_op jit(solution)/shard_map/ppermute | solution.py:35
  18.9 2.1 %collective-permute-start.5 = (bf16[256,512]{1,0:T(8,128)(2,1)S(1)}, bf16[256,512]{1,0:T(8,128)(2,1)S(1)}, u32[]{:S(2)}, u32[]{:S(2)}) collective-permute-start(bf16[256,512]{1,0:T(8,128)(2,1)S(1)} %collective-permute-done.1.refs_1_), channel_id=1, source_target_pairs={{0,16},{16,0},{32,48},{48,32},{64,80},{80,64},{96,112},{112,96},{1... | collective-permute-start | bytes 786440 | tf_op jit(solution)/shard_map/ppermute | solution.py:35
  19.4 2.0 %collective-permute-start.6 = (bf16[256,512]{1,0:T(8,128)(2,1)S(1)}, bf16[256,512]{1,0:T(8,128)(2,1)S(1)}, u32[]{:S(2)}, u32[]{:S(2)}) collective-permute-start(bf16[256,512]{1,0:T(8,128)(2,1)S(1)} %collective-permute-done.2.refs_0_), channel_id=1, source_target_pairs={{0,16},{16,0},{32,48},{48,32},{64,80},{80,64},{96,112},{112,96},{1... | collective-permute-start | bytes 786440 | tf_op jit(solution)/shard_map/ppermute | solution.py:35
  22.4 8.9 %collective-permute-start.15 = (bf16[136,512]{1,0:T(8,128)(2,1)S(1)}, bf16[136,512]{1,0:T(8,128)(2,1)S(1)}, u32[]{:S(2)}, u32[]{:S(2)}) collective-permute-start(bf16[136,512]{1,0:T(8,128)(2,1)S(1)} %get-tuple-element.45), channel_id=1, source_target_pairs={{0,2},{1,3},{2,4},{3,5},{4,6},{5,7},{6,8},{7,9},{8,10},{9,11},{10,... | collective-permute-start | bytes 417800 | tf_op jit(solution)/shard_map/ppermute | solution.py:44
  23.8 9.1 %collective-permute-start.11 = (bf16[136,512]{1,0:T(8,128)(2,1)S(1)}, bf16[136,512]{1,0:T(8,128)(2,1)S(1)}, u32[]{:S(2)}, u32[]{:S(2)}) collective-permute-start(bf16[136,512]{1,0:T(8,128)(2,1)S(1)} %get-tuple-element.39), channel_id=1, source_target_pairs={{0,14},{1,15},{2,0},{3,1},{4,2},{5,3},{6,4},{7,5},{8,6},{9,7},{10,... | collective-permute-start | bytes 417800 | tf_op jit(solution)/shard_map/ppermute | solution.py:44
  29.1 7.1 %collective-permute-start.19 = (bf16[136,512]{1,0:T(8,128)(2,1)S(1)}, bf16[136,512]{1,0:T(8,128)(2,1)S(1)}, u32[]{:S(2)}, u32[]{:S(2)}) collective-permute-start(bf16[136,512]{1,0:T(8,128)(2,1)S(1)} %get-tuple-element.48), channel_id=1, source_target_pairs={{0,14},{1,15},{2,0},{3,1},{4,2},{5,3},{6,4},{7,5},{8,6},{9,7},{10,... | collective-permute-start | bytes 417800 | tf_op jit(solution)/shard_map/ppermute | solution.py:44
  31.3 6.9 %collective-permute-start.16 = (bf16[136,512]{1,0:T(8,128)(2,1)S(1)}, bf16[136,512]{1,0:T(8,128)(2,1)S(1)}, u32[]{:S(2)}, u32[]{:S(2)}) collective-permute-start(bf16[136,512]{1,0:T(8,128)(2,1)S(1)} %add.41), channel_id=1, source_target_pairs={{0,2},{1,3},{2,4},{3,5},{4,6},{5,7},{6,8},{7,9},{8,10},{9,11},{10,... | collective-permute-start | bytes 417800 | tf_op jit(solution)/shard_map/ppermute | solution.py:44
  31.5 8.2 %collective-permute-start.8 = (bf16[136,512]{1,0:T(8,128)(2,1)S(1)}, bf16[136,512]{1,0:T(8,128)(2,1)S(1)}, u32[]{:S(2)}, u32[]{:S(2)}) collective-permute-start(bf16[136,512]{1,0:T(8,128)(2,1)S(1)} %get-tuple-element.35), channel_id=1, source_target_pairs={{0,2},{1,3},{2,4},{3,5},{4,6},{5,7},{6,8},{7,9},{8,10},{9,11},{10,... | collective-permute-start | bytes 417800 | tf_op jit(solution)/shard_map/ppermute | solution.py:44
  33.0 8.1 %collective-permute-start.12 = (bf16[136,512]{1,0:T(8,128)(2,1)S(1)}, bf16[136,512]{1,0:T(8,128)(2,1)S(1)}, u32[]{:S(2)}, u32[]{:S(2)}) collective-permute-start(bf16[136,512]{1,0:T(8,128)(2,1)S(1)} %add.38), channel_id=1, source_target_pairs={{0,14},{1,15},{2,0},{3,1},{4,2},{5,3},{6,4},{7,5},{8,6},{9,7},{10,... | collective-permute-start | bytes 417800 | tf_op jit(solution)/shard_map/ppermute | solution.py:44
  36.2 7.6 %collective-permute-start.20 = (bf16[136,512]{1,0:T(8,128)(2,1)S(1)}, bf16[136,512]{1,0:T(8,128)(2,1)S(1)}, u32[]{:S(2)}, u32[]{:S(2)}) collective-permute-start(bf16[136,512]{1,0:T(8,128)(2,1)S(1)} %add.45), channel_id=1, source_target_pairs={{0,14},{1,15},{2,0},{3,1},{4,2},{5,3},{6,4},{7,5},{8,6},{9,7},{10,... | collective-permute-start | bytes 417800 | tf_op jit(solution)/shard_map/ppermute | solution.py:44
  38.3 7.7 %collective-permute-start.17 = (bf16[136,512]{1,0:T(8,128)(2,1)S(1)}, bf16[136,512]{1,0:T(8,128)(2,1)S(1)}, u32[]{:S(2)}, u32[]{:S(2)}) collective-permute-start(bf16[136,512]{1,0:T(8,128)(2,1)S(1)} %add.42), channel_id=1, source_target_pairs={{0,2},{1,3},{2,4},{3,5},{4,6},{5,7},{6,8},{7,9},{8,10},{9,11},{10,... | collective-permute-start | bytes 417800 | tf_op jit(solution)/shard_map/ppermute | solution.py:44
  39.8 8.4 %collective-permute-start.9 = (bf16[136,512]{1,0:T(8,128)(2,1)S(1)}, bf16[136,512]{1,0:T(8,128)(2,1)S(1)}, u32[]{:S(2)}, u32[]{:S(2)}) collective-permute-start(bf16[136,512]{1,0:T(8,128)(2,1)S(1)} %add.36), channel_id=1, source_target_pairs={{0,2},{1,3},{2,4},{3,5},{4,6},{5,7},{6,8},{7,9},{8,10},{9,11},{10,... | collective-permute-start | bytes 417800 | tf_op jit(solution)/shard_map/ppermute | solution.py:44
  41.1 7.8 %collective-permute-start.13 = (bf16[136,512]{1,0:T(8,128)(2,1)S(1)}, bf16[136,512]{1,0:T(8,128)(2,1)S(1)}, u32[]{:S(2)}, u32[]{:S(2)}) collective-permute-start(bf16[136,512]{1,0:T(8,128)(2,1)S(1)} %add.39), channel_id=1, source_target_pairs={{0,14},{1,15},{2,0},{3,1},{4,2},{5,3},{6,4},{7,5},{8,6},{9,7},{10,... | collective-permute-start | bytes 417800 | tf_op jit(solution)/shard_map/ppermute | solution.py:44
  43.9 7.8 %collective-permute-start.21 = (bf16[136,512]{1,0:T(8,128)(2,1)S(1)}, bf16[136,512]{1,0:T(8,128)(2,1)S(1)}, u32[]{:S(2)}, u32[]{:S(2)}) collective-permute-start(bf16[136,512]{1,0:T(8,128)(2,1)S(1)} %add.46), channel_id=1, source_target_pairs={{0,14},{1,15},{2,0},{3,1},{4,2},{5,3},{6,4},{7,5},{8,6},{9,7},{10,... | collective-permute-start | bytes 417800 | tf_op jit(solution)/shard_map/ppermute | solution.py:44
  46.0 7.1 %collective-permute-start.18 = (bf16[136,512]{1,0:T(8,128)(2,1)S(1)}, bf16[136,512]{1,0:T(8,128)(2,1)S(1)}, u32[]{:S(2)}, u32[]{:S(2)}) collective-permute-start(bf16[136,512]{1,0:T(8,128)(2,1)S(1)} %add.43), channel_id=1, source_target_pairs={{0,2},{1,3},{2,4},{3,5},{4,6},{5,7},{6,8},{7,9},{8,10},{9,11},{10,... | collective-permute-start | bytes 417800 | tf_op jit(solution)/shard_map/ppermute | solution.py:44
  48.3 8.9 %collective-permute-start.10 = (bf16[136,512]{1,0:T(8,128)(2,1)S(1)}, bf16[136,512]{1,0:T(8,128)(2,1)S(1)}, u32[]{:S(2)}, u32[]{:S(2)}) collective-permute-start(bf16[136,512]{1,0:T(8,128)(2,1)S(1)} %add.37), channel_id=1, source_target_pairs={{0,2},{1,3},{2,4},{3,5},{4,6},{5,7},{6,8},{7,9},{8,10},{9,11},{10,... | collective-permute-start | bytes 417800 | tf_op jit(solution)/shard_map/ppermute | solution.py:44
  49.0 8.2 %collective-permute-start.14 = (bf16[136,512]{1,0:T(8,128)(2,1)S(1)}, bf16[136,512]{1,0:T(8,128)(2,1)S(1)}, u32[]{:S(2)}, u32[]{:S(2)}) collective-permute-start(bf16[136,512]{1,0:T(8,128)(2,1)S(1)} %add.40), channel_id=1, source_target_pairs={{0,14},{1,15},{2,0},{3,1},{4,2},{5,3},{6,4},{7,5},{8,6},{9,7},{10,... | collective-permute-start | bytes 417800 | tf_op jit(solution)/shard_map/ppermute | solution.py:44
  53.2 6.7 %copy-start.1 = (bf16[512,512]{1,0:T(8,128)(2,1)S(1)}, bf16[512,512]{1,0:T(8,128)(2,1)}, u32[]{:S(2)}) copy-start(bf16[512,512]{1,0:T(8,128)(2,1)} %w_neigh_ref.1) | copy-start | bytes 1572868
  53.2 6.6 %collective-permute-start.22 = (bf16[136,512]{1,0:T(8,128)(2,1)S(1)}, bf16[136,512]{1,0:T(8,128)(2,1)S(1)}, u32[]{:S(2)}, u32[]{:S(2)}) collective-permute-start(bf16[136,512]{1,0:T(8,128)(2,1)S(1)} %add_convert_fusion), channel_id=1, source_target_pairs={{0,1},{1,0},{2,3},{3,2},{4,5},{5,4},{6,7},{7,6},{8,9},{9,8},{10,11... | collective-permute-start | bytes 417800 | tf_op jit(solution)/shard_map/ppermute | solution.py:44
  (2 other events, 8.1 us)

commit v2 on v1

--- a/solution.py
+++ b/solution.py
@@ -170,11 +170,11 @@
         for x in range(len(planes)):
             out_ref = out_refs.pop(0)
             part = slice(x * TILE, (x + 1) * TILE)
-            out_ref[:TILE, :] = result[part].astype(out_ref.dtype)
+            for c in range(width // TILE):
+                columns = result[part, c * TILE : (c + 1) * TILE]
+                out_ref[c * TILE : (c + 1) * TILE, :] = columns.astype(out_ref.dtype)
             deg = jnp.sum(jnp.where(diagonal, degree[part], 0.0), axis=0, keepdims=True)
-            deg = jnp.where(mine, deg, 0.0)
-            pad = jnp.zeros((8, width - TILE), jnp.float32)
-            out_ref[TILE:, :] = jnp.concatenate([deg, pad], axis=1).astype(out_ref.dtype)
+            out_ref[width:, :] = jnp.where(mine, deg, 0.0).astype(out_ref.dtype)
 
 
 def far_sums(slots, planes, meta, a, partial, *sources):
@@ -185,7 +185,7 @@
         functools.partial(far_kernel, slots, planes),
         in_specs=[pl.BlockSpec(memory_space=pltpu.SMEM)] + [vmem] * 6,
         out_specs=[vmem] * outs,
-        out_shape=[jax.ShapeDtypeStruct((TILE + 8, width), jnp.bfloat16)] * outs,
+        out_shape=[jax.ShapeDtypeStruct((width + 8, TILE), jnp.bfloat16)] * outs,
         compiler_params=pltpu.CompilerParams(vmem_limit_bytes=8 << 20),
         cost_estimate=pl.CostEstimate(
             flops=outs * 2 * TILE * 1024 * width, transcendentals=0, bytes_accessed=outs << 19
@@ -199,8 +199,11 @@
     stale = stale_ref[...]
     hidden_ref[...] = jnp.dot(stale, w_self_ref[...], preferred_element_type=jnp.float32)
     total = sum(ref[...].astype(jnp.float32) for ref in refs[:-2])
-    total_ref[:TILE, :] = total[:TILE] + stale.astype(jnp.float32)
-    total_ref[TILE:, :] = total[TILE:]
+    width = stale.shape[1]
+    for c in range(width // TILE):
+        span = slice(c * TILE, (c + 1) * TILE)
+        total_ref[span, :] = total[span] + stale[:, span].astype(jnp.float32)
+    total_ref[width:, :] = total[width:]
 
 
 def prepare(stale, w_self, *parts):
@@ -218,10 +221,11 @@
 
 def finish_kernel(hidden_ref, total_ref, other_ref, w_neigh_ref, out_ref):
     total = total_ref[...] + other_ref[...].astype(jnp.float32)
-    scale = 1.0 / (1.0 + jnp.sum(total[TILE:, :TILE], axis=0, keepdims=True))
+    width = hidden_ref.shape[1]
+    scale = 1.0 / (1.0 + jnp.sum(total[width:], axis=0, keepdims=True))
     scale = jnp.broadcast_to(scale, (TILE, TILE)).T
-    scale = jnp.concatenate([scale] * (total.shape[1] // TILE), axis=1)
-    mean = (total[:TILE] * scale).astype(jnp.bfloat16)
+    spans = [slice(c * TILE, (c + 1) * TILE) for c in range(width // TILE)]
+    mean = jnp.concatenate([total[span] * scale for span in spans], axis=1).astype(jnp.bfloat16)
     hidden = hidden_ref[...] + jnp.dot(
         mean, w_neigh_ref[...], preferred_element_type=jnp.float32
     )

time: 62.1 us -> 61.1 us (0.984)
  no operation moved by 1% of the time
where the time goes in v2:
time: 61.1 us; the launch traced here: 59.9 us
  starting transfers between devices  33 us (54%)
  Pallas kernels  16.7 us (27%)
  waiting for transfers between devices  8.46 us (14%)
  local copies, waits for them, and re-layouts  0.94 us (2%)
    ppermute x15, starting transfers between devices, to_rep(): return lax.ppermute(value, ('blk', 'rep'), pairs)  25.6 us
    pallas_call x6, Pallas kernels, far_sums(): pl.pallas_call(functools.partial(far_kernel, slots, planes), in_specs=[pl...  6.55 us
    pallas_call x1, Pallas kernels, place_tiles(): pl.pallas_call(place_kernel, in_specs=[pl.BlockSpec(memory_space=pltpu.SM...  6.27 us
    ppermute x3, starting transfers between devices, from_pair(): return lax.ppermute(value, 'blk', pairs)  4.58 us
    ppermute x15, waiting for transfers between devices, to_rep(): return lax.ppermute(value, ('blk', 'rep'), pairs)  4.46 us
    pallas_call x2, Pallas kernels, near_sums(): pl.pallas_call(functools.partial(near_kernel, first), in_specs=[vmem] * (...  2.56 us
    ppermute x1, waiting for transfers between devices, from_single(): lax.ppermute(value, 'blk', [(blk_at(i, *SINGLE, 0), i) for i in range(16)])  2.32 us
    ppermute x1, starting transfers between devices, from_single(): lax.ppermute(value, 'blk', [(blk_at(i, *SINGLE, 0), i) for i in range(16)])  2.18 us
  transfers between devices with their start and end apart: 23, of which 8 were waited for; matrix products, arithmetic and copies ran while one was open for 2% of the time, Pallas kernels for 24%

profile of v2, /device:TPU:8, one launch (start us, length us, event | category | flops | bytes accessed | tf_op | source)
XLA Modules:
  0.0 59.9 jit_solution(12940614842128237152)
XLA Ops:
  1.6 1.6 %collective-permute-start.1 = (bf16[256,512]{1,0:T(8,128)(2,1)S(1)}, bf16[256,512]{1,0:T(8,128)(2,1)S(1)}, u32[]{:S(2)}, u32[]{:S(2)}) collective-permute-start(bf16[256,512]{1,0:T(8,128)(2,1)S(1)} %constant_dynamic-update-slice_fusion.refs_0_), channel_id=1, source_target_pairs={{128,0},{48,16},{160,32},{80,48},{192,64},{112,80},{224,96},{16,11... | collective-permute-start | bytes 786440 | tf_op jit(solution)/shard_map/ppermute | solution.py:27
  3.1 2.1 %collective-permute-start.3 = (bf16[256,512]{1,0:T(8,128)(2,1)S(1)}, bf16[256,512]{1,0:T(8,128)(2,1)S(1)}, u32[]{:S(2)}, u32[]{:S(2)}) collective-permute-start(bf16[256,512]{1,0:T(8,128)(2,1)S(1)} %constant_dynamic-update-slice_fusion.refs_0_), channel_id=1, source_target_pairs={{160,0},{112,16},{192,32},{16,48},{224,64},{48,80},{128,96},{80,11... | collective-permute-start | bytes 786440 | tf_op jit(solution)/shard_map/ppermute | solution.py:27
  6.2 2.2 %collective-permute-start.4 = (bf16[128,512]{1,0:T(8,128)(2,1)}, bf16[128,512]{1,0:T(8,128)(2,1)S(1)}, u32[]{:S(2)}, u32[]{:S(2)}) collective-permute-start(bf16[128,512]{1,0:T(8,128)(2,1)} %stale_ref.1), channel_id=1, source_target_pairs={{192,0},{208,16},{224,32},{240,48},{128,64},{144,80},{160,96},{176... | collective-permute-start | bytes 393224 | tf_op jit(solution)/shard_map/ppermute | solution.py:31
  8.4 6.3 %place_tiles.1.a_ref = bf16[16,2048,128]{2,1,0:T(8,128)(2,1)S(1)} custom-call(s32[2]{0:T(128)S(1)} %pad_add_fusion.meta, s32[16]{0:T(128)} %bitcast.9, s32[12,1,16]{2,1,0:T(1,128)} %bitcast.8, bf16[16,12,128,128]{3,2,1,0:T(8,128)(2,1)} %bitcast.7), custom_call_target="tpu_custom_call" | custom-call | flops 1048576 | bytes 14680064 | tf_op jit(solution)/shard_map/place_tiles/pallas_call | solution.py:102
  14.7 1.3 %near_sums.2.refs_2_ = f32[8,256,512]{2,1,0:T(8,128)S(1)} custom-call(bf16[16,2048,128]{2,1,0:T(8,128)(2,1)S(1)} %place_tiles.1.a_ref, bf16[256,512]{1,0:T(8,128)(2,1)S(1)} %constant_dynamic-update-slice_fusion.refs_0_, bf16[256,512]{1,0:T(8,128)(2,1)S(1)} %collective-permute-done.1.refs_1_), custom_call_target="tpu_custom_call" | custom-call | flops 1073741824 | bytes 6291456 | tf_op jit(solution)/shard_map/near_sums/pallas_call | solution.py:135
  16.0 2.3 %collective-permute-done.4.refs_0_ = bf16[128,512]{1,0:T(8,128)(2,1)S(1)} collective-permute-done((bf16[128,512]{1,0:T(8,128)(2,1)}, bf16[128,512]{1,0:T(8,128)(2,1)S(1)}, u32[]{:S(2)}, u32[]{:S(2)}) %collective-permute-start.4) | collective-permute-done | bytes 131104 | tf_op jit(solution)/shard_map/ppermute | solution.py:31
  19.5 1.3 %near_sums.3.partial_ref = f32[8,256,512]{2,1,0:T(8,128)S(1)} custom-call(bf16[16,2048,128]{2,1,0:T(8,128)(2,1)S(1)} %place_tiles.1.a_ref, bf16[256,512]{1,0:T(8,128)(2,1)S(1)} %collective-permute-done.2.refs_0_, bf16[256,512]{1,0:T(8,128)(2,1)S(1)} %collective-permute-done.3.refs_1_, f32[8,256,512]{2,1,0:T(8,128)S(1)} %near_sums.2.refs_2_), custom_call_target="tpu_custom_call" | custom-call | flops 1073741824 | bytes 6291456 | tf_op jit(solution)/shard_map/near_sums/pallas_call | solution.py:135
  21.4 1.0 %far_sums.10 = (bf16[520,128]{1,0:T(8,128)(2,1)S(1)}, bf16[520,128]{1,0:T(8,128)(2,1)S(1)}) custom-call(s32[2]{0:T(128)S(1)} %pad_add_fusion.meta, bf16[16,2048,128]{2,1,0:T(8,128)(2,1)S(1)} %place_tiles.1.a_ref, f32[8,256,512]{2,1,0:T(8,128)S(1)} %near_sums.3.partial_ref, bf16[128,512]{1,0:T(8,128)(2,1)S(1)} %collective-permute-done.4.refs_0_, ...), custom_call_target="tpu_custom_call" | custom-call | flops 268435456 | bytes 1048576 | tf_op jit(solution)/shard_map/far_sums/pallas_call | solution.py:184
  22.4 1.4 %collective-permute-start.15 = (bf16[520,128]{1,0:T(8,128)(2,1)S(1)}, bf16[520,128]{1,0:T(8,128)(2,1)S(1)}, u32[]{:S(2)}, u32[]{:S(2)}) collective-permute-start(bf16[520,128]{1,0:T(8,128)(2,1)S(1)} %get-tuple-element.45), channel_id=1, source_target_pairs={{0,2},{1,3},{2,4},{3,5},{4,6},{5,7},{6,8},{7,9},{8,10},{9,11},{10,... | collective-permute-start | bytes 399368 | tf_op jit(solution)/shard_map/ppermute | solution.py:44
  23.8 4.0 %collective-permute-start.11 = (bf16[520,128]{1,0:T(8,128)(2,1)S(1)}, bf16[520,128]{1,0:T(8,128)(2,1)S(1)}, u32[]{:S(2)}, u32[]{:S(2)}) collective-permute-start(bf16[520,128]{1,0:T(8,128)(2,1)S(1)} %get-tuple-element.39), channel_id=1, source_target_pairs={{0,14},{1,15},{2,0},{3,1},{4,2},{5,3},{6,4},{7,5},{8,6},{9,7},{10,... | collective-permute-start | bytes 399368 | tf_op jit(solution)/shard_map/ppermute | solution.py:44
  27.8 1.3 %far_sums.9 = (bf16[520,128]{1,0:T(8,128)(2,1)S(1)}, bf16[520,128]{1,0:T(8,128)(2,1)S(1)}, bf16[520,128]{1,0:T(8,128)(2,1)S(1)}, bf16[520,128]{1,0:T(8,128)(2,1)S(1)}) custom-call(s32[2]{0:T(128)S(1)} %pad_add_fusion.meta, bf16[16,2048,128]{2,1,0:T(8,128)(2,1)S(1)} %place_tiles.1.a_ref, f32[8,256,512]{2,1,0:T(8,128)S(1)} %near_sums.3.partial_ref, ...), custom_call_target="tpu_custom_call" | custom-call | flops 536870912 | bytes 2097152 | tf_op jit(solution)/shard_map/far_sums/pallas_call | solution.py:184
  29.1 2.2 %collective-permute-start.19 = (bf16[520,128]{1,0:T(8,128)(2,1)S(1)}, bf16[520,128]{1,0:T(8,128)(2,1)S(1)}, u32[]{:S(2)}, u32[]{:S(2)}) collective-permute-start(bf16[520,128]{1,0:T(8,128)(2,1)S(1)} %get-tuple-element.48), channel_id=1, source_target_pairs={{0,14},{1,15},{2,0},{3,1},{4,2},{5,3},{6,4},{7,5},{8,6},{9,7},{10,... | collective-permute-start | bytes 399368 | tf_op jit(solution)/shard_map/ppermute | solution.py:44
  31.6 1.3 %far_sums.8 = (bf16[520,128]{1,0:T(8,128)(2,1)S(1)}, bf16[520,128]{1,0:T(8,128)(2,1)S(1)}, bf16[520,128]{1,0:T(8,128)(2,1)S(1)}, bf16[520,128]{1,0:T(8,128)(2,1)S(1)}) custom-call(s32[2]{0:T(128)S(1)} %pad_add_fusion.meta, bf16[16,2048,128]{2,1,0:T(8,128)(2,1)S(1)} %place_tiles.1.a_ref, f32[8,256,512]{2,1,0:T(8,128)S(1)} %near_sums.3.partial_ref, ...), custom_call_target="tpu_custom_call" | custom-call | flops 536870912 | bytes 2097152 | tf_op jit(solution)/shard_map/far_sums/pallas_call | solution.py:184
  32.9 3.2 %collective-permute-start.12 = (bf16[520,128]{1,0:T(8,128)(2,1)S(1)}, bf16[520,128]{1,0:T(8,128)(2,1)S(1)}, u32[]{:S(2)}, u32[]{:S(2)}) collective-permute-start(bf16[520,128]{1,0:T(8,128)(2,1)S(1)} %add.38), channel_id=1, source_target_pairs={{0,14},{1,15},{2,0},{3,1},{4,2},{5,3},{6,4},{7,5},{8,6},{9,7},{10,... | collective-permute-start | bytes 399368 | tf_op jit(solution)/shard_map/ppermute | solution.py:44
  36.2 2.0 %collective-permute-start.20 = (bf16[520,128]{1,0:T(8,128)(2,1)S(1)}, bf16[520,128]{1,0:T(8,128)(2,1)S(1)}, u32[]{:S(2)}, u32[]{:S(2)}) collective-permute-start(bf16[520,128]{1,0:T(8,128)(2,1)S(1)} %add.45), channel_id=1, source_target_pairs={{0,14},{1,15},{2,0},{3,1},{4,2},{5,3},{6,4},{7,5},{8,6},{9,7},{10,... | collective-permute-start | bytes 399368 | tf_op jit(solution)/shard_map/ppermute | solution.py:44
  38.4 1.3 %far_sums.7 = (bf16[520,128]{1,0:T(8,128)(2,1)S(1)}, bf16[520,128]{1,0:T(8,128)(2,1)S(1)}, bf16[520,128]{1,0:T(8,128)(2,1)S(1)}, bf16[520,128]{1,0:T(8,128)(2,1)S(1)}) custom-call(s32[2]{0:T(128)S(1)} %pad_add_fusion.meta, bf16[16,2048,128]{2,1,0:T(8,128)(2,1)S(1)} %place_tiles.1.a_ref, f32[8,256,512]{2,1,0:T(8,128)S(1)} %near_sums.3.partial_ref, ...), custom_call_target="tpu_custom_call" | custom-call | flops 536870912 | bytes 2097152 | tf_op jit(solution)/shard_map/far_sums/pallas_call | solution.py:184
  39.8 1.1 %collective-permute-start.9 = (bf16[520,128]{1,0:T(8,128)(2,1)S(1)}, bf16[520,128]{1,0:T(8,128)(2,1)S(1)}, u32[]{:S(2)}, u32[]{:S(2)}) collective-permute-start(bf16[520,128]{1,0:T(8,128)(2,1)S(1)} %add.36), channel_id=1, source_target_pairs={{0,2},{1,3},{2,4},{3,5},{4,6},{5,7},{6,8},{7,9},{8,10},{9,11},{10,... | collective-permute-start | bytes 399368 | tf_op jit(solution)/shard_map/ppermute | solution.py:44
  40.9 2.5 %collective-permute-start.13 = (bf16[520,128]{1,0:T(8,128)(2,1)S(1)}, bf16[520,128]{1,0:T(8,128)(2,1)S(1)}, u32[]{:S(2)}, u32[]{:S(2)}) collective-permute-start(bf16[520,128]{1,0:T(8,128)(2,1)S(1)} %add.39), channel_id=1, source_target_pairs={{0,14},{1,15},{2,0},{3,1},{4,2},{5,3},{6,4},{7,5},{8,6},{9,7},{10,... | collective-permute-start | bytes 399368 | tf_op jit(solution)/shard_map/ppermute | solution.py:44
  43.5 2.1 %collective-permute-start.21 = (bf16[520,128]{1,0:T(8,128)(2,1)S(1)}, bf16[520,128]{1,0:T(8,128)(2,1)S(1)}, u32[]{:S(2)}, u32[]{:S(2)}) collective-permute-start(bf16[520,128]{1,0:T(8,128)(2,1)S(1)} %add.46), channel_id=1, source_target_pairs={{0,14},{1,15},{2,0},{3,1},{4,2},{5,3},{6,4},{7,5},{8,6},{9,7},{10,... | collective-permute-start | bytes 399368 | tf_op jit(solution)/shard_map/ppermute | solution.py:44
  46.6 1.1 %collective-permute-done.9 = bf16[520,128]{1,0:T(8,128)(2,1)S(1)} collective-permute-done((bf16[520,128]{1,0:T(8,128)(2,1)S(1)}, bf16[520,128]{1,0:T(8,128)(2,1)S(1)}, u32[]{:S(2)}, u32[]{:S(2)}) %collective-permute-start.9) | collective-permute-done | bytes 133152 | tf_op jit(solution)/shard_map/ppermute | solution.py:44
  48.6 2.6 %collective-permute-start.14 = (bf16[520,128]{1,0:T(8,128)(2,1)S(1)}, bf16[520,128]{1,0:T(8,128)(2,1)S(1)}, u32[]{:S(2)}, u32[]{:S(2)}) collective-permute-start(bf16[520,128]{1,0:T(8,128)(2,1)S(1)} %add.40), channel_id=1, source_target_pairs={{0,14},{1,15},{2,0},{3,1},{4,2},{5,3},{6,4},{7,5},{8,6},{9,7},{10,... | collective-permute-start | bytes 399368 | tf_op jit(solution)/shard_map/ppermute | solution.py:44
  52.3 3.1 %collective-permute-start.22 = (bf16[520,128]{1,0:T(8,128)(2,1)S(1)}, bf16[520,128]{1,0:T(8,128)(2,1)S(1)}, u32[]{:S(2)}, u32[]{:S(2)}) collective-permute-start(bf16[520,128]{1,0:T(8,128)(2,1)S(1)} %add_convert_fusion), channel_id=1, source_target_pairs={{0,1},{1,0},{2,3},{3,2},{4,5},{5,4},{6,7},{7,6},{8,9},{9,8},{10,11... | collective-permute-start | bytes 399368 | tf_op jit(solution)/shard_map/ppermute | solution.py:44
  56.5 2.3 %collective-permute-done.22.other_ref = bf16[520,128]{1,0:T(8,128)(2,1)S(1)} collective-permute-done((bf16[520,128]{1,0:T(8,128)(2,1)S(1)}, bf16[520,128]{1,0:T(8,128)(2,1)S(1)}, u32[]{:S(2)}, u32[]{:S(2)}) %collective-permute-start.22) | collective-permute-done | bytes 133152 | tf_op jit(solution)/shard_map/ppermute | solution.py:44
  58.8 1.0 %finish.1 = bf16[128,512]{1,0:T(8,128)(2,1)} custom-call(f32[128,512]{1,0:T(8,128)S(1)} %get-tuple-element.40.hidden_ref, f32[520,128]{1,0:T(8,128)S(1)} %get-tuple-element.41.total_ref, bf16[520,128]{1,0:T(8,128)(2,1)S(1)} %collective-permute-done.22.other_ref, bf16[512,512]{1,0:T(8,128)(2,1)S(1)} %copy-done), custom_call_target="tpu_custom_call" | custom-call | tf_op jit(solution)/shard_map/finish/pallas_call | solution.py:238
  (54 shorter events, 9.0 us)
Async XLA Ops:
  0.0 1.6 %collective-permute-start = (bf16[128,512]{1,0:T(8,128)(2,1)}, bf16[128,512]{1,0:T(8,128)(2,1)S(1)}, u32[]{:S(2)}, u32[]{:S(2)}) collective-permute-start(bf16[128,512]{1,0:T(8,128)(2,1)} %stale_ref.1), channel_id=1, source_target_pairs={{0,16},{16,0},{32,48},{48,32},{64,80},{80,64},{96,112},{112,96},{1... | collective-permute-start | bytes 393224 | tf_op jit(solution)/shard_map/ppermute | solution.py:35
  1.6 13.1 %collective-permute-start.1 = (bf16[256,512]{1,0:T(8,128)(2,1)S(1)}, bf16[256,512]{1,0:T(8,128)(2,1)S(1)}, u32[]{:S(2)}, u32[]{:S(2)}) collective-permute-start(bf16[256,512]{1,0:T(8,128)(2,1)S(1)} %constant_dynamic-update-slice_fusion.refs_0_), channel_id=1, source_target_pairs={{128,0},{48,16},{160,32},{80,48},{192,64},{112,80},{224,96},{16,11... | collective-permute-start | bytes 786440 | tf_op jit(solution)/shard_map/ppermute | solution.py:27
  3.1 15.1 %collective-permute-start.3 = (bf16[256,512]{1,0:T(8,128)(2,1)S(1)}, bf16[256,512]{1,0:T(8,128)(2,1)S(1)}, u32[]{:S(2)}, u32[]{:S(2)}) collective-permute-start(bf16[256,512]{1,0:T(8,128)(2,1)S(1)} %constant_dynamic-update-slice_fusion.refs_0_), channel_id=1, source_target_pairs={{160,0},{112,16},{192,32},{16,48},{224,64},{48,80},{128,96},{80,11... | collective-permute-start | bytes 786440 | tf_op jit(solution)/shard_map/ppermute | solution.py:27
  5.3 13.5 %collective-permute-start.2 = (bf16[256,512]{1,0:T(8,128)(2,1)S(1)}, bf16[256,512]{1,0:T(8,128)(2,1)S(1)}, u32[]{:S(2)}, u32[]{:S(2)}) collective-permute-start(bf16[256,512]{1,0:T(8,128)(2,1)S(1)} %constant_dynamic-update-slice_fusion.refs_0_), channel_id=1, source_target_pairs={{64,0},{240,16},{96,32},{144,48},{0,64},{176,80},{32,96},{208,112}... | collective-permute-start | bytes 786440 | tf_op jit(solution)/shard_map/ppermute | solution.py:27
  6.2 12.1 %collective-permute-start.4 = (bf16[128,512]{1,0:T(8,128)(2,1)}, bf16[128,512]{1,0:T(8,128)(2,1)S(1)}, u32[]{:S(2)}, u32[]{:S(2)}) collective-permute-start(bf16[128,512]{1,0:T(8,128)(2,1)} %stale_ref.1), channel_id=1, source_target_pairs={{192,0},{208,16},{224,32},{240,48},{128,64},{144,80},{160,96},{176... | collective-permute-start | bytes 393224 | tf_op jit(solution)/shard_map/ppermute | solution.py:31
  18.8 2.6 %collective-permute-start.7 = (bf16[384,512]{1,0:T(8,128)(2,1)S(1)}, bf16[384,512]{1,0:T(8,128)(2,1)S(1)}, u32[]{:S(2)}, u32[]{:S(2)}) collective-permute-start(bf16[384,512]{1,0:T(8,128)(2,1)S(1)} %pad_maximum_fusion), channel_id=1, source_target_pairs={{0,16},{16,0},{32,48},{48,32},{64,80},{80,64},{96,112},{112,96},{1... | collective-permute-start | bytes 1179656 | tf_op jit(solution)/shard_map/ppermute | solution.py:35
  18.9 2.1 %collective-permute-start.5 = (bf16[256,512]{1,0:T(8,128)(2,1)S(1)}, bf16[256,512]{1,0:T(8,128)(2,1)S(1)}, u32[]{:S(2)}, u32[]{:S(2)}) collective-permute-start(bf16[256,512]{1,0:T(8,128)(2,1)S(1)} %collective-permute-done.1.refs_1_), channel_id=1, source_target_pairs={{0,16},{16,0},{32,48},{48,32},{64,80},{80,64},{96,112},{112,96},{1... | collective-permute-start | bytes 786440 | tf_op jit(solution)/shard_map/ppermute | solution.py:35
  19.4 2.0 %collective-permute-start.6 = (bf16[256,512]{1,0:T(8,128)(2,1)S(1)}, bf16[256,512]{1,0:T(8,128)(2,1)S(1)}, u32[]{:S(2)}, u32[]{:S(2)}) collective-permute-start(bf16[256,512]{1,0:T(8,128)(2,1)S(1)} %collective-permute-done.2.refs_0_), channel_id=1, source_target_pairs={{0,16},{16,0},{32,48},{48,32},{64,80},{80,64},{96,112},{112,96},{1... | collective-permute-start | bytes 786440 | tf_op jit(solution)/shard_map/ppermute | solution.py:35
  22.4 8.9 %collective-permute-start.15 = (bf16[520,128]{1,0:T(8,128)(2,1)S(1)}, bf16[520,128]{1,0:T(8,128)(2,1)S(1)}, u32[]{:S(2)}, u32[]{:S(2)}) collective-permute-start(bf16[520,128]{1,0:T(8,128)(2,1)S(1)} %get-tuple-element.45), channel_id=1, source_target_pairs={{0,2},{1,3},{2,4},{3,5},{4,6},{5,7},{6,8},{7,9},{8,10},{9,11},{10,... | collective-permute-start | bytes 399368 | tf_op jit(solution)/shard_map/ppermute | solution.py:44
  23.8 9.1 %collective-permute-start.11 = (bf16[520,128]{1,0:T(8,128)(2,1)S(1)}, bf16[520,128]{1,0:T(8,128)(2,1)S(1)}, u32[]{:S(2)}, u32[]{:S(2)}) collective-permute-start(bf16[520,128]{1,0:T(8,128)(2,1)S(1)} %get-tuple-element.39), channel_id=1, source_target_pairs={{0,14},{1,15},{2,0},{3,1},{4,2},{5,3},{6,4},{7,5},{8,6},{9,7},{10,... | collective-permute-start | bytes 399368 | tf_op jit(solution)/shard_map/ppermute | solution.py:44
  29.1 7.1 %collective-permute-start.19 = (bf16[520,128]{1,0:T(8,128)(2,1)S(1)}, bf16[520,128]{1,0:T(8,128)(2,1)S(1)}, u32[]{:S(2)}, u32[]{:S(2)}) collective-permute-start(bf16[520,128]{1,0:T(8,128)(2,1)S(1)} %get-tuple-element.48), channel_id=1, source_target_pairs={{0,14},{1,15},{2,0},{3,1},{4,2},{5,3},{6,4},{7,5},{8,6},{9,7},{10,... | collective-permute-start | bytes 399368 | tf_op jit(solution)/shard_map/ppermute | solution.py:44
  31.3 6.9 %collective-permute-start.16 = (bf16[520,128]{1,0:T(8,128)(2,1)S(1)}, bf16[520,128]{1,0:T(8,128)(2,1)S(1)}, u32[]{:S(2)}, u32[]{:S(2)}) collective-permute-start(bf16[520,128]{1,0:T(8,128)(2,1)S(1)} %add.41), channel_id=1, source_target_pairs={{0,2},{1,3},{2,4},{3,5},{4,6},{5,7},{6,8},{7,9},{8,10},{9,11},{10,... | collective-permute-start | bytes 399368 | tf_op jit(solution)/shard_map/ppermute | solution.py:44
  31.5 8.2 %collective-permute-start.8 = (bf16[520,128]{1,0:T(8,128)(2,1)S(1)}, bf16[520,128]{1,0:T(8,128)(2,1)S(1)}, u32[]{:S(2)}, u32[]{:S(2)}) collective-permute-start(bf16[520,128]{1,0:T(8,128)(2,1)S(1)} %get-tuple-element.35), channel_id=1, source_target_pairs={{0,2},{1,3},{2,4},{3,5},{4,6},{5,7},{6,8},{7,9},{8,10},{9,11},{10,... | collective-permute-start | bytes 399368 | tf_op jit(solution)/shard_map/ppermute | solution.py:44
  32.9 8.0 %collective-permute-start.12 = (bf16[520,128]{1,0:T(8,128)(2,1)S(1)}, bf16[520,128]{1,0:T(8,128)(2,1)S(1)}, u32[]{:S(2)}, u32[]{:S(2)}) collective-permute-start(bf16[520,128]{1,0:T(8,128)(2,1)S(1)} %add.38), channel_id=1, source_target_pairs={{0,14},{1,15},{2,0},{3,1},{4,2},{5,3},{6,4},{7,5},{8,6},{9,7},{10,... | collective-permute-start | bytes 399368 | tf_op jit(solution)/shard_map/ppermute | solution.py:44
  36.2 7.2 %collective-permute-start.20 = (bf16[520,128]{1,0:T(8,128)(2,1)S(1)}, bf16[520,128]{1,0:T(8,128)(2,1)S(1)}, u32[]{:S(2)}, u32[]{:S(2)}) collective-permute-start(bf16[520,128]{1,0:T(8,128)(2,1)S(1)} %add.45), channel_id=1, source_target_pairs={{0,14},{1,15},{2,0},{3,1},{4,2},{5,3},{6,4},{7,5},{8,6},{9,7},{10,... | collective-permute-start | bytes 399368 | tf_op jit(solution)/shard_map/ppermute | solution.py:44
  38.3 7.3 %collective-permute-start.17 = (bf16[520,128]{1,0:T(8,128)(2,1)S(1)}, bf16[520,128]{1,0:T(8,128)(2,1)S(1)}, u32[]{:S(2)}, u32[]{:S(2)}) collective-permute-start(bf16[520,128]{1,0:T(8,128)(2,1)S(1)} %add.42), channel_id=1, source_target_pairs={{0,2},{1,3},{2,4},{3,5},{4,6},{5,7},{6,8},{7,9},{8,10},{9,11},{10,... | collective-permute-start | bytes 399368 | tf_op jit(solution)/shard_map/ppermute | solution.py:44
  39.8 7.9 %collective-permute-start.9 = (bf16[520,128]{1,0:T(8,128)(2,1)S(1)}, bf16[520,128]{1,0:T(8,128)(2,1)S(1)}, u32[]{:S(2)}, u32[]{:S(2)}) collective-permute-start(bf16[520,128]{1,0:T(8,128)(2,1)S(1)} %add.36), channel_id=1, source_target_pairs={{0,2},{1,3},{2,4},{3,5},{4,6},{5,7},{6,8},{7,9},{8,10},{9,11},{10,... | collective-permute-start | bytes 399368 | tf_op jit(solution)/shard_map/ppermute | solution.py:44
  40.9 7.6 %collective-permute-start.13 = (bf16[520,128]{1,0:T(8,128)(2,1)S(1)}, bf16[520,128]{1,0:T(8,128)(2,1)S(1)}, u32[]{:S(2)}, u32[]{:S(2)}) collective-permute-start(bf16[520,128]{1,0:T(8,128)(2,1)S(1)} %add.39), channel_id=1, source_target_pairs={{0,14},{1,15},{2,0},{3,1},{4,2},{5,3},{6,4},{7,5},{8,6},{9,7},{10,... | collective-permute-start | bytes 399368 | tf_op jit(solution)/shard_map/ppermute | solution.py:44
  43.5 7.7 %collective-permute-start.21 = (bf16[520,128]{1,0:T(8,128)(2,1)S(1)}, bf16[520,128]{1,0:T(8,128)(2,1)S(1)}, u32[]{:S(2)}, u32[]{:S(2)}) collective-permute-start(bf16[520,128]{1,0:T(8,128)(2,1)S(1)} %add.46), channel_id=1, source_target_pairs={{0,14},{1,15},{2,0},{3,1},{4,2},{5,3},{6,4},{7,5},{8,6},{9,7},{10,... | collective-permute-start | bytes 399368 | tf_op jit(solution)/shard_map/ppermute | solution.py:44
  45.6 6.5 %collective-permute-start.18 = (bf16[520,128]{1,0:T(8,128)(2,1)S(1)}, bf16[520,128]{1,0:T(8,128)(2,1)S(1)}, u32[]{:S(2)}, u32[]{:S(2)}) collective-permute-start(bf16[520,128]{1,0:T(8,128)(2,1)S(1)} %add.43), channel_id=1, source_target_pairs={{0,2},{1,3},{2,4},{3,5},{4,6},{5,7},{6,8},{7,9},{8,10},{9,11},{10,... | collective-permute-start | bytes 399368 | tf_op jit(solution)/shard_map/ppermute | solution.py:44
  47.7 8.5 %collective-permute-start.10 = (bf16[520,128]{1,0:T(8,128)(2,1)S(1)}, bf16[520,128]{1,0:T(8,128)(2,1)S(1)}, u32[]{:S(2)}, u32[]{:S(2)}) collective-permute-start(bf16[520,128]{1,0:T(8,128)(2,1)S(1)} %add.37), channel_id=1, source_target_pairs={{0,2},{1,3},{2,4},{3,5},{4,6},{5,7},{6,8},{7,9},{8,10},{9,11},{10,... | collective-permute-start | bytes 399368 | tf_op jit(solution)/shard_map/ppermute | solution.py:44
  48.6 7.6 %collective-permute-start.14 = (bf16[520,128]{1,0:T(8,128)(2,1)S(1)}, bf16[520,128]{1,0:T(8,128)(2,1)S(1)}, u32[]{:S(2)}, u32[]{:S(2)}) collective-permute-start(bf16[520,128]{1,0:T(8,128)(2,1)S(1)} %add.40), channel_id=1, source_target_pairs={{0,14},{1,15},{2,0},{3,1},{4,2},{5,3},{6,4},{7,5},{8,6},{9,7},{10,... | collective-permute-start | bytes 399368 | tf_op jit(solution)/shard_map/ppermute | solution.py:44
  52.2 6.6 %copy-start = (bf16[512,512]{1,0:T(8,128)(2,1)S(1)}, bf16[512,512]{1,0:T(8,128)(2,1)}, u32[]{:S(2)}) copy-start(bf16[512,512]{1,0:T(8,128)(2,1)} %w_neigh_ref.1) | copy-start | bytes 1572868
  52.3 6.6 %collective-permute-start.22 = (bf16[520,128]{1,0:T(8,128)(2,1)S(1)}, bf16[520,128]{1,0:T(8,128)(2,1)S(1)}, u32[]{:S(2)}, u32[]{:S(2)}) collective-permute-start(bf16[520,128]{1,0:T(8,128)(2,1)S(1)} %add_convert_fusion), channel_id=1, source_target_pairs={{0,1},{1,0},{2,3},{3,2},{4,5},{5,4},{6,7},{7,6},{8,9},{9,8},{10,11... | collective-permute-start | bytes 399368 | tf_op jit(solution)/shard_map/ppermute | solution.py:44
  (2 other events, 8.1 us)
